TPU v7x, 512 devices: a whole 4x4x16 slice. The times are simulated.
512 devices in a mesh: tm: 64 (over y, x, z_lo), freq: 8 (over z_hi, core).
Axes of the slice: x: 4, y: 4, z: 16 (z_hi: 4, z_lo: 4; z = z_hi * 4 + z_lo), core: 2. Of those that a mesh axis runs over, the one named last changes fastest.
Arguments:
- features: bfloat16 [512, 256, 256], P('tm', 'freq'), may hold values from -6 to 6
- upstream: bfloat16 [512, 256, 256], P('tm', 'freq'), may hold values from -6 to 6
- weights: bfloat16 [8, 256, 256], replicated, may hold values from -8 to 8
- gains: float32 [2, 256], replicated, may hold values from 0.5 to 1.5
Outputs:
- grad_input: bfloat16 [512, 256, 256], P('tm', 'freq')
- weight_grads: float32 [8, 256, 256], replicated
- gain_grads: float32 [2, 256], replicated
All inputs are finite; a program needn't handle non-finite values.
Results may differ from a plain program's by a relative error of at most 0.02.
Values may be sent and summed in bfloat16 or wider, within the bound.
A program may use at most 128 MiB of HBM per device.

v0:
```python
import jax
import jax.numpy as jnp
from jax import lax
from jax.sharding import PartitionSpec as P

HEADS = 4
WINDOW = 128


epsilon = 1e-06
masked_score = -1e30


def passed_along(block, axis, distance):
    devices = range(lax.axis_size(axis))
    route = [(i - distance, i) for i in devices if i - distance in devices]
    return lax.ppermute(block, axis, route)


def norm_forward(inputs, gain):
    widened = inputs.astype(jnp.float32)
    inverse = lax.rsqrt(jnp.mean(widened * widened, axis=-1, keepdims=True) + epsilon)
    unit_rows = widened * inverse
    return ((unit_rows * gain).astype(jnp.bfloat16), inverse, unit_rows)


def norm_backward(incoming, inverse, unit_rows, gain):
    scaled = incoming * gain
    result = inverse * (scaled - unit_rows * jnp.mean(scaled * unit_rows, axis=-1, keepdims=True))
    gain_grad = jnp.sum((incoming * unit_rows).reshape(-1, unit_rows.shape[-1]), axis=0)
    return (result, gain_grad)


def project(inputs, matrix):
    flat_rows = inputs.reshape(-1, inputs.shape[-1])
    product = jnp.dot(flat_rows, matrix, preferred_element_type=jnp.float32)
    return product.reshape(inputs.shape[:-1] + (matrix.shape[1],))


def project_back(grads, matrices):
    running = jnp.zeros((grads[0].size // grads[0].shape[-1], matrices[0].shape[0]), jnp.float32)
    for grad_part, matrix in zip(grads, matrices):
        flat_rows = grad_part.reshape(-1, grad_part.shape[-1])
        running = running + lax.dot_general(
            flat_rows, matrix, (((1,), (1,)), ((), ())), preferred_element_type=jnp.float32
        )
    return running.reshape(grads[0].shape[:-1] + (matrices[0].shape[0],))


def weight_grad(inputs, grads):
    return lax.dot_general(
        inputs.reshape(-1, inputs.shape[-1]),
        grads.reshape(-1, grads.shape[-1]),
        (((0,), (0,)), ((), ())),
        preferred_element_type=jnp.float32,
    )


def channel_masks(width, ndim, dtype):
    owner = jnp.arange(width, dtype=jnp.int32)[None, :] // (width // HEADS)
    chosen = (owner == jnp.arange(HEADS, dtype=jnp.int32)[:, None]).astype(dtype)
    return chosen.reshape((HEADS,) + (1,) * ndim + (width,))


def spread_heads(rows):
    return rows[None] * channel_masks(rows.shape[-1], rows.ndim - 1, rows.dtype)


def collect_heads(stacked):
    return jnp.sum(
        stacked * channel_masks(stacked.shape[-1], stacked.ndim - 2, jnp.float32), axis=0
    )


def head_scale(rows):
    return (rows.shape[-1] // HEADS) ** (-0.5)


def attend(queries, key_rows, value_rows, allowed, query_form, key_form):
    scaling = head_scale(queries)
    scores = (
        jnp.einsum(
            "h" + query_form + "," + key_form + "->bhqk",
            spread_heads(queries),
            key_rows,
            preferred_element_type=jnp.float32,
        )
        * scaling
    )
    scores = jnp.where(allowed, scores, masked_score)
    largest = jnp.max(scores, axis=-1, keepdims=True)
    log_total = largest + jnp.log(jnp.sum(jnp.exp(scores - largest), axis=-1, keepdims=True))
    attention = jnp.exp(scores - log_total)
    stacked = jnp.einsum(
        "bhqk," + key_form + "->h" + query_form,
        attention.astype(jnp.bfloat16),
        value_rows,
        preferred_element_type=jnp.float32,
    )
    mixed_rows = collect_heads(stacked).astype(jnp.bfloat16)
    return (mixed_rows, log_total[..., 0], attention)


def query_backward(attention, grad_out, key_rows, value_rows, query_form, key_form):
    scaling = head_scale(key_rows)
    grad_attention = jnp.einsum(
        "h" + query_form + "," + key_form + "->bhqk",
        spread_heads(grad_out),
        value_rows,
        preferred_element_type=jnp.float32,
    )
    row_dot = jnp.sum(grad_attention * attention, axis=-1, keepdims=True)
    grad_scores = (attention * (grad_attention - row_dot) * scaling).astype(jnp.bfloat16)
    stacked = jnp.einsum(
        "bhqk," + key_form + "->h" + query_form,
        grad_scores,
        key_rows,
        preferred_element_type=jnp.float32,
    )
    grad_queries = collect_heads(stacked).astype(jnp.bfloat16)
    return (grad_queries, row_dot[..., 0], grad_scores)


def key_terms(attention, grad_scores, queries, grad_out, query_form, key_form):
    grad_keys = collect_heads(
        jnp.einsum(
            "bhqk," + query_form + "->h" + key_form,
            grad_scores,
            queries,
            preferred_element_type=jnp.float32,
        )
    )
    grad_values = collect_heads(
        jnp.einsum(
            "bhqk," + query_form + "->h" + key_form,
            attention.astype(jnp.bfloat16),
            grad_out,
            preferred_element_type=jnp.float32,
        )
    )
    return (grad_keys, grad_values)


def key_backward(
    queries, grad_out, log_total, row_dot, key_rows, value_rows, allowed, query_form, key_form
):
    scaling = head_scale(key_rows)
    scores = (
        jnp.einsum(
            query_form + ",h" + key_form + "->bhqk",
            queries,
            spread_heads(key_rows),
            preferred_element_type=jnp.float32,
        )
        * scaling
    )
    scores = jnp.where(allowed, scores, masked_score)
    attention = jnp.exp(scores - log_total[..., None])
    grad_attention = jnp.einsum(
        query_form + ",h" + key_form + "->bhqk",
        grad_out,
        spread_heads(value_rows),
        preferred_element_type=jnp.float32,
    )
    grad_scores = (attention * (grad_attention - row_dot[..., None]) * scaling).astype(jnp.bfloat16)
    return key_terms(attention, grad_scores, queries, grad_out, query_form, key_form)


def window_masks(first_frame, frames_dev, window, total_frames):
    half_window = window // 2
    row_ids = jnp.arange(frames_dev, dtype=jnp.int32)[:, None]
    col_ids = jnp.arange(frames_dev + window, dtype=jnp.int32)[None, :]
    frame_ids = first_frame - half_window + col_ids
    inside = (frame_ids >= 0) & (frame_ids < total_frames)
    distance = col_ids - row_ids
    ahead_mask = (distance >= 0) & (distance < window) & inside
    behind_mask = (distance.T >= 1) & (distance.T <= window) & inside.T
    return (ahead_mask, behind_mask)


def per_device(features, upstream, weights, gains):
    frames_dev = features.shape[0]
    bins_dev = features.shape[1]
    total_frames = frames_dev * lax.axis_size("tm")
    hops = WINDOW // 2 // frames_dev
    lower_rows = hops * frames_dev
    first_frame = lax.axis_index("tm") * frames_dev
    ahead_mask, behind_mask = window_masks(first_frame, frames_dev, WINDOW, total_frames)
    window_offsets = [offset for offset in range(-hops, hops + 1) if offset != 0]
    norm_one, inverse_one, unit_one = norm_forward(features, gains[0])
    query_one = project(norm_one, weights[0]).astype(jnp.bfloat16)
    key_one = project(norm_one, weights[1]).astype(jnp.bfloat16)
    value_one = project(norm_one, weights[2]).astype(jnp.bfloat16)
    moved = (
        lax.all_to_all(query_one, "freq", split_axis=0, concat_axis=1, tiled=True),
        lax.all_to_all(key_one, "freq", split_axis=0, concat_axis=1, tiled=True),
        lax.all_to_all(value_one, "freq", split_axis=0, concat_axis=1, tiled=True),
    )
    frame_query = moved[0]
    frame_key = moved[1]
    frame_value = moved[2]
    freq_out, _, freq_attention = attend(frame_query, frame_key, frame_value, True, "bqc", "bkc")
    mixed_one = lax.all_to_all(freq_out, "freq", split_axis=1, concat_axis=0, tiled=True)
    hidden = (features.astype(jnp.float32) + project(mixed_one, weights[3])).astype(jnp.bfloat16)
    norm_two, inverse_two, unit_two = norm_forward(hidden, gains[1])
    query_two = project(norm_two, weights[4]).astype(jnp.bfloat16)
    key_two = project(norm_two, weights[5]).astype(jnp.bfloat16)
    value_two = project(norm_two, weights[6]).astype(jnp.bfloat16)
    arrived = [
        passed_along((query_two, key_two, value_two), "tm", -offset) for offset in window_offsets
    ]
    remote_query = jnp.concatenate([piece[0] for piece in arrived], axis=0)
    remote_key = jnp.concatenate([piece[1] for piece in arrived], axis=0)
    remote_value = jnp.concatenate([piece[2] for piece in arrived], axis=0)

    def windowed(remote_rows, local_rows):
        return jnp.concatenate(
            [remote_rows[:lower_rows], local_rows, remote_rows[lower_rows:]], axis=0
        )

    window_query = windowed(remote_query, query_two)
    window_key = windowed(remote_key, key_two)
    window_value = windowed(remote_value, value_two)
    mixed_two, log_two, time_attention = attend(
        query_two, window_key, window_value, ahead_mask[None, None], "qbc", "kbc"
    )
    grad_mixed_two = project_back([upstream], [weights[7]]).astype(jnp.bfloat16)
    grad_query_two, row_two, _ = query_backward(
        time_attention, grad_mixed_two, window_key, window_value, "qbc", "kbc"
    )
    grad_arrived = [passed_along(grad_mixed_two, "tm", -offset) for offset in window_offsets]
    stats_arrived = [passed_along((log_two, row_two), "tm", -offset) for offset in window_offsets]
    remote_grad = jnp.concatenate(grad_arrived, axis=0)
    remote_log = jnp.concatenate([piece[0] for piece in stats_arrived], axis=2)
    remote_row = jnp.concatenate([piece[1] for piece in stats_arrived], axis=2)
    window_grad = windowed(remote_grad, grad_mixed_two)
    window_log = jnp.concatenate(
        [remote_log[:, :, :lower_rows], log_two, remote_log[:, :, lower_rows:]], axis=2
    )
    window_row = jnp.concatenate(
        [remote_row[:, :, :lower_rows], row_two, remote_row[:, :, lower_rows:]], axis=2
    )
    grad_key_two, grad_value_two = key_backward(
        window_query,
        window_grad,
        window_log,
        window_row,
        key_two,
        value_two,
        behind_mask[None, None],
        "qbc",
        "kbc",
    )
    grad_key_two = grad_key_two.astype(jnp.bfloat16)
    grad_value_two = grad_value_two.astype(jnp.bfloat16)
    grad_norm_two = project_back(
        [grad_query_two, grad_key_two, grad_value_two], [weights[4], weights[5], weights[6]]
    )
    hidden_part, gain_two = norm_backward(grad_norm_two, inverse_two, unit_two, gains[1])
    grad_hidden = (upstream.astype(jnp.float32) + hidden_part).astype(jnp.bfloat16)
    time_stack = jnp.stack(
        [
            weight_grad(norm_two, grad_query_two),
            weight_grad(norm_two, grad_key_two),
            weight_grad(norm_two, grad_value_two),
            weight_grad(mixed_two, upstream),
        ]
    )
    grad_mixed_one = project_back([grad_hidden], [weights[3]]).astype(jnp.bfloat16)
    frame_grad = lax.all_to_all(grad_mixed_one, "freq", split_axis=0, concat_axis=1, tiled=True)
    grad_frame_query, _, grad_scores = query_backward(
        freq_attention, frame_grad, frame_key, frame_value, "bqc", "bkc"
    )
    grad_frame_key, grad_frame_value = key_terms(
        freq_attention, grad_scores, frame_query, frame_grad, "bqc", "bkc"
    )
    returned = (
        lax.all_to_all(grad_frame_query, "freq", split_axis=1, concat_axis=0, tiled=True),
        lax.all_to_all(
            grad_frame_key.astype(jnp.bfloat16), "freq", split_axis=1, concat_axis=0, tiled=True
        ),
        lax.all_to_all(
            grad_frame_value.astype(jnp.bfloat16), "freq", split_axis=1, concat_axis=0, tiled=True
        ),
    )
    grad_norm_one = project_back(
        [returned[0], returned[1], returned[2]], [weights[0], weights[1], weights[2]]
    )
    input_part, gain_one = norm_backward(grad_norm_one, inverse_one, unit_one, gains[0])
    grad_input = (grad_hidden.astype(jnp.float32) + input_part).astype(jnp.bfloat16)
    freq_stack = jnp.stack(
        [
            weight_grad(norm_one, returned[0]),
            weight_grad(norm_one, returned[1]),
            weight_grad(norm_one, returned[2]),
            weight_grad(mixed_one, grad_hidden),
        ]
    )
    summed = lax.psum(
        (jnp.concatenate([freq_stack, time_stack], axis=0), jnp.stack([gain_one, gain_two])),
        ("tm", "freq"),
    )
    weight_grads = summed[0]
    gain_grads = summed[1]
    inv_root = (total_frames * bins_dev * lax.axis_size("freq")) ** (-0.5)
    return (grad_input, weight_grads * inv_root, gain_grads * inv_root)


def solution(mesh):
    return jax.shard_map(
        per_device,
        mesh=mesh,
        in_specs=(P("tm", "freq", None), P("tm", "freq", None), P(), P()),
        out_specs=(P("tm", "freq", None), P(), P()),
        check_vma=False,
    )
```

profile of v0, /device:TPU:1, one launch (start us, length us, event | category | flops | bytes accessed | tf_op | source)
XLA Modules:
  0.0 1130.1 jit_solution(9239675720553322760)
XLA Ops:
  8.4 5.5 collective-permute-start.64
  13.8 6.3 collective-permute-start.65
  34.8 15.4 %all-to-all-start.2 = ((bf16[8,32,256]{2,1,0:T(8,128)(2,1)}), bf16[8,32,256]{2,1,0:T(8,128)(2,1)S(1)}, u32[]{:S(2)}, u32[]{:S(2)}) async-start(bf16[8,32,256]{2,1,0:T(8,128)(2,1)} %convolution_convert_fusion.5), calls=%async_computation.2 | async-start | bytes 262144 | tf_op jit(solution)/shard_map/all_to_all | solution.py:196
  56.1 5.3 collective-permute-start.69
  73.1 4.8 collective-permute-done.72
  79.2 11.9 %all-to-all-start.1 = ((bf16[8,32,256]{2,1,0:T(8,128)(2,1)}), bf16[8,32,256]{2,1,0:T(8,128)(2,1)S(1)}, u32[]{:S(2)}, u32[]{:S(2)}) async-start(bf16[8,32,256]{2,1,0:T(8,128)(2,1)} %convolution_convert_fusion.6), calls=%async_computation.1 | async-start | bytes 262144 | tf_op jit(solution)/shard_map/all_to_all | solution.py:195
  96.4 8.1 all-to-all-done.1
  104.5 7.2 all-to-all-start
  112.2 15.2 %all-to-all-done = bf16[8,32,256]{2,1,0:T(8,128)(2,1)S(1)} async-done(((bf16[8,32,256]{2,1,0:T(8,128)(2,1)}), bf16[8,32,256]{2,1,0:T(8,128)(2,1)S(1)}, u32[]{:S(2)}, u32[]{:S(2)}) %all-to-all-start) | async-done | bytes 131104 | tf_op jit(solution)/shard_map/all_to_all | solution.py:197
  131.4 5.1 all-to-all-start.3
  139.2 12.4 %all-to-all-done.3 = bf16[8,2,4096]{2,1,0:T(2,128)(2,1)S(1)} async-done(((bf16[8,2,4096]{2,1,0:T(2,128)(2,1)}), bf16[8,2,4096]{2,1,0:T(2,128)(2,1)S(1)}, u32[]{:S(2)}, u32[]{:S(2)}) %all-to-all-start.3) | async-done | bytes 131104 | tf_op jit(solution)/shard_map/all_to_all | solution.py:203
  153.0 9.5 collective-permute-start
  163.8 12.9 %collective-permute-start.2 = (bf16[8,32,256]{2,1,0:T(8,128)(2,1)S(1)}, bf16[8,32,256]{2,1,0:T(8,128)(2,1)S(1)}, u32[]{:S(2)}, u32[]{:S(2)}) collective-permute-start(bf16[8,32,256]{2,1,0:T(8,128)(2,1)S(1)} %convolution_convert_fusion.4), channel_id=1, source_target_pairs={{0,48},{8,56},{16,64},{24,72},{32,80},{40,88},{48,96},{56,104},{64... | collective-permute-start | bytes 393224 | tf_op jit(solution)/shard_map/ppermute | solution.py:17
  186.7 7.0 collective-permute-start.5
  210.3 7.5 collective-permute-done.9
  220.5 5.5 collective-permute-start.16
  226.0 6.7 collective-permute-start.17
  235.4 5.8 collective-permute-start.19
  246.9 7.9 collective-permute-start.21
  268.4 9.9 collective-permute-done.25
  281.0 5.5 collective-permute-start.32
  286.6 6.7 collective-permute-start.33
  293.3 5.4 collective-permute-start.34
  298.8 4.5 collective-permute-start.35
  303.4 5.3 collective-permute-start.36
  315.9 6.1 collective-permute-start.37
  342.0 6.1 collective-permute-done.41
  352.0 9.7 collective-permute-start.48
  361.8 5.7 collective-permute-start.49
  368.2 7.6 collective-permute-start.50
  375.8 4.5 collective-permute-start.51
  380.3 5.2 collective-permute-start.52
  385.5 6.1 collective-permute-start.53
  413.6 11.4 %collective-permute-start.80 = (f32[32,4,8]{2,1,0:T(4,128)}, f32[32,4,8]{2,1,0:T(4,128)S(1)}, u32[]{:S(2)}, u32[]{:S(2)}) collective-permute-start(f32[32,4,8]{2,1,0:T(4,128)} %get-tuple-element.17), channel_id=1, source_target_pairs={{0,64},{8,72},{16,80},{24,88},{32,96},{40,104},{48,112},{56,120},{... | collective-permute-start | bytes 12296 | tf_op jit(solution)/shard_map/ppermute | solution.py:17
  425.7 6.4 collective-permute-start.81
  432.0 8.2 collective-permute-start.82
  440.2 4.6 collective-permute-start.83
  444.8 5.2 collective-permute-start.84
  450.6 6.1 collective-permute-start.85
  497.1 6.2 fusion.85
  510.0 38.9 %all_to_all.32 = bf16[8,32,256]{2,1,0:T(8,128)(2,1)S(1)} all-to-all(bf16[8,32,256]{2,1,0:T(8,128)(2,1)S(1)} %convolution_convert_fusion), channel_id=1, replica_groups=mesh['tm'=64,'freq'=8] {'freq'}, dimensions={0} | all-to-all | bytes 262144 | tf_op jit(solution)/shard_map/all_to_all | solution.py:270
  557.9 5.7 all-to-all-start.5
  578.0 8.8 all-to-all-start.6
  590.3 9.5 all-to-all-done.6
  599.8 7.4 all-to-all-start.7
  612.3 9.4 all-to-all-done.7
  631.7 114.6 %psum.15 = f32[2,256]{1,0:T(2,128)S(1)} all-reduce(f32[2,256]{1,0:T(2,128)S(1)} %pad_maximum_fusion), channel_id=1, replica_groups=mesh['tm'=64,'freq'=8] {'tm','freq'}, use_global_device_ids=true, to_apply=%region_21.22 | all-reduce | flops 512 | bytes 4096 | tf_op jit(solution)/shard_map/psum | solution.py:299
  748.7 371.5 %all-reduce.2.cloned.1.call-done = f32[8,256,256]{2,1,0:T(8,128)} async-done(((f32[8,256,256]{2,1,0:T(8,128)}), f32[8,256,256]{2,1,0:T(8,128)}) %all-reduce.2.cloned.1.call-update) | async-done | bytes 2097168 | tf_op jit(solution)/shard_map/psum | solution.py:299
  (422 shorter events, 251.3 us)
Async XLA Ops:
  8.4 47.8 %collective-permute-start.64 = (bf16[8,32,256]{2,1,0:T(8,128)(2,1)S(1)}, bf16[8,32,256]{2,1,0:T(8,128)(2,1)S(1)}, u32[]{:S(2)}, u32[]{:S(2)}) collective-permute-start(bf16[8,32,256]{2,1,0:T(8,128)(2,1)S(1)} %convolution_convert_fusion.2), channel_id=1, source_target_pairs={{0,64},{8,72},{16,80},{24,88},{32,96},{40,104},{48,112},{56,120},{... | collective-permute-start | bytes 393224 | tf_op jit(solution)/shard_map/ppermute | solution.py:17
  13.8 47.7 %collective-permute-start.65 = (bf16[8,32,256]{2,1,0:T(8,128)(2,1)S(1)}, bf16[8,32,256]{2,1,0:T(8,128)(2,1)S(1)}, u32[]{:S(2)}, u32[]{:S(2)}) collective-permute-start(bf16[8,32,256]{2,1,0:T(8,128)(2,1)S(1)} %convolution_convert_fusion.2), channel_id=1, source_target_pairs={{0,56},{8,64},{16,72},{24,80},{32,88},{40,96},{48,104},{56,112},{6... | collective-permute-start | bytes 393224 | tf_op jit(solution)/shard_map/ppermute | solution.py:17
  20.1 43.0 %collective-permute-start.66 = (bf16[8,32,256]{2,1,0:T(8,128)(2,1)S(1)}, bf16[8,32,256]{2,1,0:T(8,128)(2,1)S(1)}, u32[]{:S(2)}, u32[]{:S(2)}) collective-permute-start(bf16[8,32,256]{2,1,0:T(8,128)(2,1)S(1)} %convolution_convert_fusion.2), channel_id=1, source_target_pairs={{0,48},{8,56},{16,64},{24,72},{32,80},{40,88},{48,96},{56,104},{64... | collective-permute-start | bytes 393224 | tf_op jit(solution)/shard_map/ppermute | solution.py:17
  22.4 44.0 %collective-permute-start.67 = (bf16[8,32,256]{2,1,0:T(8,128)(2,1)S(1)}, bf16[8,32,256]{2,1,0:T(8,128)(2,1)S(1)}, u32[]{:S(2)}, u32[]{:S(2)}) collective-permute-start(bf16[8,32,256]{2,1,0:T(8,128)(2,1)S(1)} %convolution_convert_fusion.2), channel_id=1, source_target_pairs={{0,40},{8,48},{16,56},{24,64},{32,72},{40,80},{48,88},{56,96},{64,... | collective-permute-start | bytes 393224 | tf_op jit(solution)/shard_map/ppermute | solution.py:17
  26.9 40.9 %collective-permute-start.68 = (bf16[8,32,256]{2,1,0:T(8,128)(2,1)S(1)}, bf16[8,32,256]{2,1,0:T(8,128)(2,1)S(1)}, u32[]{:S(2)}, u32[]{:S(2)}) collective-permute-start(bf16[8,32,256]{2,1,0:T(8,128)(2,1)S(1)} %convolution_convert_fusion.2), channel_id=1, source_target_pairs={{0,32},{8,40},{16,48},{24,56},{32,64},{40,72},{48,80},{56,88},{64,... | collective-permute-start | bytes 393224 | tf_op jit(solution)/shard_map/ppermute | solution.py:17
  34.8 44.4 %all-to-all-start.2 = ((bf16[8,32,256]{2,1,0:T(8,128)(2,1)}), bf16[8,32,256]{2,1,0:T(8,128)(2,1)S(1)}, u32[]{:S(2)}, u32[]{:S(2)}) async-start(bf16[8,32,256]{2,1,0:T(8,128)(2,1)} %convolution_convert_fusion.5), calls=%async_computation.2 | async-start | bytes 262144 | tf_op jit(solution)/shard_map/all_to_all | solution.py:196
  67.8 24.1 %collective-permute-start.73 = (bf16[8,32,256]{2,1,0:T(8,128)(2,1)S(1)}, bf16[8,32,256]{2,1,0:T(8,128)(2,1)S(1)}, u32[]{:S(2)}, u32[]{:S(2)}) collective-permute-start(bf16[8,32,256]{2,1,0:T(8,128)(2,1)S(1)} %convolution_convert_fusion.2), channel_id=1, source_target_pairs={{16,0},{24,8},{32,16},{40,24},{48,32},{56,40},{64,48},{72,56},{80,... | collective-permute-start | bytes 393224 | tf_op jit(solution)/shard_map/ppermute | solution.py:17
  69.1 24.7 %collective-permute-start.74 = (bf16[8,32,256]{2,1,0:T(8,128)(2,1)S(1)}, bf16[8,32,256]{2,1,0:T(8,128)(2,1)S(1)}, u32[]{:S(2)}, u32[]{:S(2)}) collective-permute-start(bf16[8,32,256]{2,1,0:T(8,128)(2,1)S(1)} %convolution_convert_fusion.2), channel_id=1, source_target_pairs={{24,0},{32,8},{40,16},{48,24},{56,32},{64,40},{72,48},{80,56},{88,... | collective-permute-start | bytes 393224 | tf_op jit(solution)/shard_map/ppermute | solution.py:17
  70.4 25.4 %collective-permute-start.75 = (bf16[8,32,256]{2,1,0:T(8,128)(2,1)S(1)}, bf16[8,32,256]{2,1,0:T(8,128)(2,1)S(1)}, u32[]{:S(2)}, u32[]{:S(2)}) collective-permute-start(bf16[8,32,256]{2,1,0:T(8,128)(2,1)S(1)} %convolution_convert_fusion.2), channel_id=1, source_target_pairs={{32,0},{40,8},{48,16},{56,24},{64,32},{72,40},{80,48},{88,56},{96,... | collective-permute-start | bytes 393224 | tf_op jit(solution)/shard_map/ppermute | solution.py:17
  71.7 64.7 %collective-permute-start.76 = (bf16[8,32,256]{2,1,0:T(8,128)(2,1)S(1)}, bf16[8,32,256]{2,1,0:T(8,128)(2,1)S(1)}, u32[]{:S(2)}, u32[]{:S(2)}) collective-permute-start(bf16[8,32,256]{2,1,0:T(8,128)(2,1)S(1)} %convolution_convert_fusion.2), channel_id=1, source_target_pairs={{40,0},{48,8},{56,16},{64,24},{72,32},{80,40},{88,48},{96,56},{104... | collective-permute-start | bytes 393224 | tf_op jit(solution)/shard_map/ppermute | solution.py:17
  77.9 59.2 %collective-permute-start.77 = (bf16[8,32,256]{2,1,0:T(8,128)(2,1)S(1)}, bf16[8,32,256]{2,1,0:T(8,128)(2,1)S(1)}, u32[]{:S(2)}, u32[]{:S(2)}) collective-permute-start(bf16[8,32,256]{2,1,0:T(8,128)(2,1)S(1)} %convolution_convert_fusion.2), channel_id=1, source_target_pairs={{48,0},{56,8},{64,16},{72,24},{80,32},{88,40},{96,48},{104,56},{11... | collective-permute-start | bytes 393224 | tf_op jit(solution)/shard_map/ppermute | solution.py:17
  79.2 25.3 %all-to-all-start.1 = ((bf16[8,32,256]{2,1,0:T(8,128)(2,1)}), bf16[8,32,256]{2,1,0:T(8,128)(2,1)S(1)}, u32[]{:S(2)}, u32[]{:S(2)}) async-start(bf16[8,32,256]{2,1,0:T(8,128)(2,1)} %convolution_convert_fusion.6), calls=%async_computation.1 | async-start | bytes 262144 | tf_op jit(solution)/shard_map/all_to_all | solution.py:195
  91.8 46.0 %collective-permute-start.78 = (bf16[8,32,256]{2,1,0:T(8,128)(2,1)S(1)}, bf16[8,32,256]{2,1,0:T(8,128)(2,1)S(1)}, u32[]{:S(2)}, u32[]{:S(2)}) collective-permute-start(bf16[8,32,256]{2,1,0:T(8,128)(2,1)S(1)} %convolution_convert_fusion.2), channel_id=1, source_target_pairs={{56,0},{64,8},{72,16},{80,24},{88,32},{96,40},{104,48},{112,56},{1... | collective-permute-start | bytes 393224 | tf_op jit(solution)/shard_map/ppermute | solution.py:17
  93.8 44.7 %collective-permute-start.79 = (bf16[8,32,256]{2,1,0:T(8,128)(2,1)S(1)}, bf16[8,32,256]{2,1,0:T(8,128)(2,1)S(1)}, u32[]{:S(2)}, u32[]{:S(2)}) collective-permute-start(bf16[8,32,256]{2,1,0:T(8,128)(2,1)S(1)} %convolution_convert_fusion.2), channel_id=1, source_target_pairs={{64,0},{72,8},{80,16},{88,24},{96,32},{104,40},{112,48},{120,56},{... | collective-permute-start | bytes 393224 | tf_op jit(solution)/shard_map/ppermute | solution.py:17
  104.5 22.9 %all-to-all-start = ((bf16[8,32,256]{2,1,0:T(8,128)(2,1)}), bf16[8,32,256]{2,1,0:T(8,128)(2,1)S(1)}, u32[]{:S(2)}, u32[]{:S(2)}) async-start(bf16[8,32,256]{2,1,0:T(8,128)(2,1)} %convolution_convert_fusion.7), calls=%async_computation | async-start | bytes 262144 | tf_op jit(solution)/shard_map/all_to_all | solution.py:197
  153.0 33.7 %collective-permute-start = (bf16[8,32,256]{2,1,0:T(8,128)(2,1)S(1)}, bf16[8,32,256]{2,1,0:T(8,128)(2,1)S(1)}, u32[]{:S(2)}, u32[]{:S(2)}) collective-permute-start(bf16[8,32,256]{2,1,0:T(8,128)(2,1)S(1)} %convolution_convert_fusion.4), channel_id=1, source_target_pairs={{0,64},{8,72},{16,80},{24,88},{32,96},{40,104},{48,112},{56,120},{... | collective-permute-start | bytes 393224 | tf_op jit(solution)/shard_map/ppermute | solution.py:17
  162.5 31.2 %collective-permute-start.1 = (bf16[8,32,256]{2,1,0:T(8,128)(2,1)S(1)}, bf16[8,32,256]{2,1,0:T(8,128)(2,1)S(1)}, u32[]{:S(2)}, u32[]{:S(2)}) collective-permute-start(bf16[8,32,256]{2,1,0:T(8,128)(2,1)S(1)} %convolution_convert_fusion.4), channel_id=1, source_target_pairs={{0,56},{8,64},{16,72},{24,80},{32,88},{40,96},{48,104},{56,112},{6... | collective-permute-start | bytes 393224 | tf_op jit(solution)/shard_map/ppermute | solution.py:17
  163.8 31.3 %collective-permute-start.2 = (bf16[8,32,256]{2,1,0:T(8,128)(2,1)S(1)}, bf16[8,32,256]{2,1,0:T(8,128)(2,1)S(1)}, u32[]{:S(2)}, u32[]{:S(2)}) collective-permute-start(bf16[8,32,256]{2,1,0:T(8,128)(2,1)S(1)} %convolution_convert_fusion.4), channel_id=1, source_target_pairs={{0,48},{8,56},{16,64},{24,72},{32,80},{40,88},{48,96},{56,104},{64... | collective-permute-start | bytes 393224 | tf_op jit(solution)/shard_map/ppermute | solution.py:17
  203.3 22.8 %collective-permute-start.12 = (bf16[8,32,256]{2,1,0:T(8,128)(2,1)S(1)}, bf16[8,32,256]{2,1,0:T(8,128)(2,1)S(1)}, u32[]{:S(2)}, u32[]{:S(2)}) collective-permute-start(bf16[8,32,256]{2,1,0:T(8,128)(2,1)S(1)} %convolution_convert_fusion.4), channel_id=1, source_target_pairs={{40,0},{48,8},{56,16},{64,24},{72,32},{80,40},{88,48},{96,56},{104... | collective-permute-start | bytes 393224 | tf_op jit(solution)/shard_map/ppermute | solution.py:17
  209.0 23.8 %collective-permute-start.13 = (bf16[8,32,256]{2,1,0:T(8,128)(2,1)S(1)}, bf16[8,32,256]{2,1,0:T(8,128)(2,1)S(1)}, u32[]{:S(2)}, u32[]{:S(2)}) collective-permute-start(bf16[8,32,256]{2,1,0:T(8,128)(2,1)S(1)} %convolution_convert_fusion.4), channel_id=1, source_target_pairs={{48,0},{56,8},{64,16},{72,24},{80,32},{88,40},{96,48},{104,56},{11... | collective-permute-start | bytes 393224 | tf_op jit(solution)/shard_map/ppermute | solution.py:17
  220.5 26.4 %collective-permute-start.16 = (bf16[8,32,256]{2,1,0:T(8,128)(2,1)S(1)}, bf16[8,32,256]{2,1,0:T(8,128)(2,1)S(1)}, u32[]{:S(2)}, u32[]{:S(2)}) collective-permute-start(bf16[8,32,256]{2,1,0:T(8,128)(2,1)S(1)} %convolution_convert_fusion.1), channel_id=1, source_target_pairs={{0,64},{8,72},{16,80},{24,88},{32,96},{40,104},{48,112},{56,120},{... | collective-permute-start | bytes 393224 | tf_op jit(solution)/shard_map/ppermute | solution.py:17
  226.0 28.9 %collective-permute-start.17 = (bf16[8,32,256]{2,1,0:T(8,128)(2,1)S(1)}, bf16[8,32,256]{2,1,0:T(8,128)(2,1)S(1)}, u32[]{:S(2)}, u32[]{:S(2)}) collective-permute-start(bf16[8,32,256]{2,1,0:T(8,128)(2,1)S(1)} %convolution_convert_fusion.1), channel_id=1, source_target_pairs={{0,56},{8,64},{16,72},{24,80},{32,88},{40,96},{48,104},{56,112},{6... | collective-permute-start | bytes 393224 | tf_op jit(solution)/shard_map/ppermute | solution.py:17
  232.8 24.7 %collective-permute-start.18 = (bf16[8,32,256]{2,1,0:T(8,128)(2,1)S(1)}, bf16[8,32,256]{2,1,0:T(8,128)(2,1)S(1)}, u32[]{:S(2)}, u32[]{:S(2)}) collective-permute-start(bf16[8,32,256]{2,1,0:T(8,128)(2,1)S(1)} %convolution_convert_fusion.1), channel_id=1, source_target_pairs={{0,48},{8,56},{16,64},{24,72},{32,80},{40,88},{48,96},{56,104},{64... | collective-permute-start | bytes 393224 | tf_op jit(solution)/shard_map/ppermute | solution.py:17
  235.4 23.6 %collective-permute-start.19 = (bf16[8,32,256]{2,1,0:T(8,128)(2,1)S(1)}, bf16[8,32,256]{2,1,0:T(8,128)(2,1)S(1)}, u32[]{:S(2)}, u32[]{:S(2)}) collective-permute-start(bf16[8,32,256]{2,1,0:T(8,128)(2,1)S(1)} %convolution_convert_fusion.1), channel_id=1, source_target_pairs={{0,40},{8,48},{16,56},{24,64},{32,72},{40,80},{48,88},{56,96},{64,... | collective-permute-start | bytes 393224 | tf_op jit(solution)/shard_map/ppermute | solution.py:17
  264.4 22.2 %collective-permute-start.28 = (bf16[8,32,256]{2,1,0:T(8,128)(2,1)S(1)}, bf16[8,32,256]{2,1,0:T(8,128)(2,1)S(1)}, u32[]{:S(2)}, u32[]{:S(2)}) collective-permute-start(bf16[8,32,256]{2,1,0:T(8,128)(2,1)S(1)} %convolution_convert_fusion.1), channel_id=1, source_target_pairs={{40,0},{48,8},{56,16},{64,24},{72,32},{80,40},{88,48},{96,56},{104... | collective-permute-start | bytes 393224 | tf_op jit(solution)/shard_map/ppermute | solution.py:17
  267.1 26.2 %collective-permute-start.29 = (bf16[8,32,256]{2,1,0:T(8,128)(2,1)S(1)}, bf16[8,32,256]{2,1,0:T(8,128)(2,1)S(1)}, u32[]{:S(2)}, u32[]{:S(2)}) collective-permute-start(bf16[8,32,256]{2,1,0:T(8,128)(2,1)S(1)} %convolution_convert_fusion.1), channel_id=1, source_target_pairs={{48,0},{56,8},{64,16},{72,24},{80,32},{88,40},{96,48},{104,56},{11... | collective-permute-start | bytes 393224 | tf_op jit(solution)/shard_map/ppermute | solution.py:17
  279.7 23.6 %collective-permute-start.31 = (bf16[8,32,256]{2,1,0:T(8,128)(2,1)S(1)}, bf16[8,32,256]{2,1,0:T(8,128)(2,1)S(1)}, u32[]{:S(2)}, u32[]{:S(2)}) collective-permute-start(bf16[8,32,256]{2,1,0:T(8,128)(2,1)S(1)} %convolution_convert_fusion.1), channel_id=1, source_target_pairs={{64,0},{72,8},{80,16},{88,24},{96,32},{104,40},{112,48},{120,56},{... | collective-permute-start | bytes 393224 | tf_op jit(solution)/shard_map/ppermute | solution.py:17
  281.0 34.9 %collective-permute-start.32 = (bf16[8,32,256]{2,1,0:T(8,128)(2,1)S(1)}, bf16[8,32,256]{2,1,0:T(8,128)(2,1)S(1)}, u32[]{:S(2)}, u32[]{:S(2)}) collective-permute-start(bf16[8,32,256]{2,1,0:T(8,128)(2,1)S(1)} %convolution_convert_fusion.3), channel_id=1, source_target_pairs={{0,64},{8,72},{16,80},{24,88},{32,96},{40,104},{48,112},{56,120},{... | collective-permute-start | bytes 393224 | tf_op jit(solution)/shard_map/ppermute | solution.py:17
  286.6 36.1 %collective-permute-start.33 = (bf16[8,32,256]{2,1,0:T(8,128)(2,1)S(1)}, bf16[8,32,256]{2,1,0:T(8,128)(2,1)S(1)}, u32[]{:S(2)}, u32[]{:S(2)}) collective-permute-start(bf16[8,32,256]{2,1,0:T(8,128)(2,1)S(1)} %convolution_convert_fusion.3), channel_id=1, source_target_pairs={{0,56},{8,64},{16,72},{24,80},{32,88},{40,96},{48,104},{56,112},{6... | collective-permute-start | bytes 393224 | tf_op jit(solution)/shard_map/ppermute | solution.py:17
  293.3 34.3 %collective-permute-start.34 = (bf16[8,32,256]{2,1,0:T(8,128)(2,1)S(1)}, bf16[8,32,256]{2,1,0:T(8,128)(2,1)S(1)}, u32[]{:S(2)}, u32[]{:S(2)}) collective-permute-start(bf16[8,32,256]{2,1,0:T(8,128)(2,1)S(1)} %convolution_convert_fusion.3), channel_id=1, source_target_pairs={{0,48},{8,56},{16,64},{24,72},{32,80},{40,88},{48,96},{56,104},{64... | collective-permute-start | bytes 393224 | tf_op jit(solution)/shard_map/ppermute | solution.py:17
  298.8 30.8 %collective-permute-start.35 = (bf16[8,32,256]{2,1,0:T(8,128)(2,1)S(1)}, bf16[8,32,256]{2,1,0:T(8,128)(2,1)S(1)}, u32[]{:S(2)}, u32[]{:S(2)}) collective-permute-start(bf16[8,32,256]{2,1,0:T(8,128)(2,1)S(1)} %convolution_convert_fusion.3), channel_id=1, source_target_pairs={{0,40},{8,48},{16,56},{24,64},{32,72},{40,80},{48,88},{56,96},{64,... | collective-permute-start | bytes 393224 | tf_op jit(solution)/shard_map/ppermute | solution.py:17
  303.4 28.2 %collective-permute-start.36 = (bf16[8,32,256]{2,1,0:T(8,128)(2,1)S(1)}, bf16[8,32,256]{2,1,0:T(8,128)(2,1)S(1)}, u32[]{:S(2)}, u32[]{:S(2)}) collective-permute-start(bf16[8,32,256]{2,1,0:T(8,128)(2,1)S(1)} %convolution_convert_fusion.3), channel_id=1, source_target_pairs={{0,32},{8,40},{16,48},{24,56},{32,64},{40,72},{48,80},{56,88},{64,... | collective-permute-start | bytes 393224 | tf_op jit(solution)/shard_map/ppermute | solution.py:17
  337.4 24.3 %collective-permute-start.44 = (bf16[8,32,256]{2,1,0:T(8,128)(2,1)S(1)}, bf16[8,32,256]{2,1,0:T(8,128)(2,1)S(1)}, u32[]{:S(2)}, u32[]{:S(2)}) collective-permute-start(bf16[8,32,256]{2,1,0:T(8,128)(2,1)S(1)} %convolution_convert_fusion.3), channel_id=1, source_target_pairs={{40,0},{48,8},{56,16},{64,24},{72,32},{80,40},{88,48},{96,56},{104... | collective-permute-start | bytes 393224 | tf_op jit(solution)/shard_map/ppermute | solution.py:17
  340.0 28.2 %collective-permute-start.45 = (bf16[8,32,256]{2,1,0:T(8,128)(2,1)S(1)}, bf16[8,32,256]{2,1,0:T(8,128)(2,1)S(1)}, u32[]{:S(2)}, u32[]{:S(2)}) collective-permute-start(bf16[8,32,256]{2,1,0:T(8,128)(2,1)S(1)} %convolution_convert_fusion.3), channel_id=1, source_target_pairs={{48,0},{56,8},{64,16},{72,24},{80,32},{88,40},{96,48},{104,56},{11... | collective-permute-start | bytes 393224 | tf_op jit(solution)/shard_map/ppermute | solution.py:17
  348.1 27.6 %collective-permute-start.46 = (bf16[8,32,256]{2,1,0:T(8,128)(2,1)S(1)}, bf16[8,32,256]{2,1,0:T(8,128)(2,1)S(1)}, u32[]{:S(2)}, u32[]{:S(2)}) collective-permute-start(bf16[8,32,256]{2,1,0:T(8,128)(2,1)S(1)} %convolution_convert_fusion.3), channel_id=1, source_target_pairs={{56,0},{64,8},{72,16},{80,24},{88,32},{96,40},{104,48},{112,56},{1... | collective-permute-start | bytes 393224 | tf_op jit(solution)/shard_map/ppermute | solution.py:17
  350.1 30.2 %collective-permute-start.47 = (bf16[8,32,256]{2,1,0:T(8,128)(2,1)S(1)}, bf16[8,32,256]{2,1,0:T(8,128)(2,1)S(1)}, u32[]{:S(2)}, u32[]{:S(2)}) collective-permute-start(bf16[8,32,256]{2,1,0:T(8,128)(2,1)S(1)} %convolution_convert_fusion.3), channel_id=1, source_target_pairs={{64,0},{72,8},{80,16},{88,24},{96,32},{104,40},{112,48},{120,56},{... | collective-permute-start | bytes 393224 | tf_op jit(solution)/shard_map/ppermute | solution.py:17
  352.0 33.5 %collective-permute-start.48 = (f32[32,4,8]{2,1,0:T(4,128)S(1)}, f32[32,4,8]{2,1,0:T(4,128)S(1)}, u32[]{:S(2)}, u32[]{:S(2)}) collective-permute-start(f32[32,4,8]{2,1,0:T(4,128)S(1)} %bitcast.299), channel_id=1, source_target_pairs={{0,64},{8,72},{16,80},{24,88},{32,96},{40,104},{48,112},{56,120},{... | collective-permute-start | bytes 12296 | tf_op jit(solution)/shard_map/ppermute | solution.py:17
  361.8 29.9 %collective-permute-start.49 = (f32[32,4,8]{2,1,0:T(4,128)S(1)}, f32[32,4,8]{2,1,0:T(4,128)S(1)}, u32[]{:S(2)}, u32[]{:S(2)}) collective-permute-start(f32[32,4,8]{2,1,0:T(4,128)S(1)} %bitcast.300), channel_id=1, source_target_pairs={{0,56},{8,64},{16,72},{24,80},{32,88},{40,96},{48,104},{56,112},{6... | collective-permute-start | bytes 12296 | tf_op jit(solution)/shard_map/ppermute | solution.py:17
  368.2 28.4 %collective-permute-start.50 = (f32[32,4,8]{2,1,0:T(4,128)S(1)}, f32[32,4,8]{2,1,0:T(4,128)S(1)}, u32[]{:S(2)}, u32[]{:S(2)}) collective-permute-start(f32[32,4,8]{2,1,0:T(4,128)S(1)} %bitcast.301), channel_id=1, source_target_pairs={{0,48},{8,56},{16,64},{24,72},{32,80},{40,88},{48,96},{56,104},{64... | collective-permute-start | bytes 12296 | tf_op jit(solution)/shard_map/ppermute | solution.py:17
  405.1 26.9 %collective-permute-start.61 = (f32[32,4,8]{2,1,0:T(4,128)S(1)}, f32[32,4,8]{2,1,0:T(4,128)S(1)}, u32[]{:S(2)}, u32[]{:S(2)}) collective-permute-start(f32[32,4,8]{2,1,0:T(4,128)S(1)} %bitcast.312), channel_id=1, source_target_pairs={{48,0},{56,8},{64,16},{72,24},{80,32},{88,40},{96,48},{104,56},{11... | collective-permute-start | bytes 12296 | tf_op jit(solution)/shard_map/ppermute | solution.py:17
  407.2 33.0 %collective-permute-start.62 = (f32[32,4,8]{2,1,0:T(4,128)S(1)}, f32[32,4,8]{2,1,0:T(4,128)S(1)}, u32[]{:S(2)}, u32[]{:S(2)}) collective-permute-start(f32[32,4,8]{2,1,0:T(4,128)S(1)} %bitcast.313), channel_id=1, source_target_pairs={{56,0},{64,8},{72,16},{80,24},{88,32},{96,40},{104,48},{112,56},{1... | collective-permute-start | bytes 12296 | tf_op jit(solution)/shard_map/ppermute | solution.py:17
  410.7 34.1 %collective-permute-start.63 = (f32[32,4,8]{2,1,0:T(4,128)S(1)}, f32[32,4,8]{2,1,0:T(4,128)S(1)}, u32[]{:S(2)}, u32[]{:S(2)}) collective-permute-start(f32[32,4,8]{2,1,0:T(4,128)S(1)} %bitcast.314), channel_id=1, source_target_pairs={{64,0},{72,8},{80,16},{88,24},{96,32},{104,40},{112,48},{120,56},{... | collective-permute-start | bytes 12296 | tf_op jit(solution)/shard_map/ppermute | solution.py:17
  413.6 36.4 %collective-permute-start.80 = (f32[32,4,8]{2,1,0:T(4,128)}, f32[32,4,8]{2,1,0:T(4,128)S(1)}, u32[]{:S(2)}, u32[]{:S(2)}) collective-permute-start(f32[32,4,8]{2,1,0:T(4,128)} %get-tuple-element.17), channel_id=1, source_target_pairs={{0,64},{8,72},{16,80},{24,88},{32,96},{40,104},{48,112},{56,120},{... | collective-permute-start | bytes 12296 | tf_op jit(solution)/shard_map/ppermute | solution.py:17
  425.7 34.3 %collective-permute-start.81 = (f32[32,4,8]{2,1,0:T(4,128)}, f32[32,4,8]{2,1,0:T(4,128)}, u32[]{:S(2)}, u32[]{:S(2)}) collective-permute-start(f32[32,4,8]{2,1,0:T(4,128)} %get-tuple-element.17), channel_id=1, source_target_pairs={{0,56},{8,64},{16,72},{24,80},{32,88},{40,96},{48,104},{56,112},{6... | collective-permute-start | bytes 12296 | tf_op jit(solution)/shard_map/ppermute | solution.py:17
  432.0 32.3 %collective-permute-start.82 = (f32[32,4,8]{2,1,0:T(4,128)}, f32[32,4,8]{2,1,0:T(4,128)}, u32[]{:S(2)}, u32[]{:S(2)}) collective-permute-start(f32[32,4,8]{2,1,0:T(4,128)} %get-tuple-element.17), channel_id=1, source_target_pairs={{0,48},{8,56},{16,64},{24,72},{32,80},{40,88},{48,96},{56,104},{64... | collective-permute-start | bytes 12296 | tf_op jit(solution)/shard_map/ppermute | solution.py:17
  440.2 26.0 %collective-permute-start.83 = (f32[32,4,8]{2,1,0:T(4,128)}, f32[32,4,8]{2,1,0:T(4,128)}, u32[]{:S(2)}, u32[]{:S(2)}) collective-permute-start(f32[32,4,8]{2,1,0:T(4,128)} %get-tuple-element.17), channel_id=1, source_target_pairs={{0,40},{8,48},{16,56},{24,64},{32,72},{40,80},{48,88},{56,96},{64,... | collective-permute-start | bytes 12296 | tf_op jit(solution)/shard_map/ppermute | solution.py:17
  444.8 22.7 %collective-permute-start.84 = (f32[32,4,8]{2,1,0:T(4,128)}, f32[32,4,8]{2,1,0:T(4,128)}, u32[]{:S(2)}, u32[]{:S(2)}) collective-permute-start(f32[32,4,8]{2,1,0:T(4,128)} %get-tuple-element.17), channel_id=1, source_target_pairs={{0,32},{8,40},{16,48},{24,56},{32,64},{40,72},{48,80},{56,88},{64,... | collective-permute-start | bytes 12296 | tf_op jit(solution)/shard_map/ppermute | solution.py:17
  607.2 512.9 %all-reduce.2.cloned.1.call-start = ((), (), s32[]{:S(2)}) async-start(), calls=%async_computation.8 | async-start | bytes 4194304 | tf_op jit(solution)/shard_map/psum | solution.py:299
  (108 other events, 2370.1 us)
Sparse Core Ops, SparseCore 0:
  630.4 489.7 all-reduce.1
where the time goes:
time: 1130 us
  waiting for transfers between devices  481 us (43%)
  starting transfers between devices  366 us (32%)
  blocking collectives  154 us (14%)
  matrix products  52.5 us (5%)
  local copies, waits for them, and re-layouts  42.2 us (4%)
  other arithmetic  19.1 us (2%)
  between operations  16.3 us (1%)
    psum x1, waiting for transfers between devices, per_device(): lax.psum((jnp.concatenate([freq_stack, time_stack], axis=0), jnp.stack([g...  371 us
    ppermute x96, starting transfers between devices, passed_along(): return lax.ppermute(block, axis, route)  304 us
    psum x1, blocking collectives, per_device(): lax.psum((jnp.concatenate([freq_stack, time_stack], axis=0), jnp.stack([g...  115 us
    ppermute x96, waiting for transfers between devices, passed_along(): return lax.ppermute(block, axis, route)  51.6 us
    all_to_all x1, blocking collectives, per_device(): lax.all_to_all(grad_mixed_one, 'freq', split_axis=0, concat_axis=1, tiled...  38.9 us
    unnamed x178, local copies, waits for them, and re-layouts  28.9 us
  transfers between devices with their start and end apart: 104, of which 21 were waited for; matrix products, arithmetic and copies ran while one was open for 6% of the time, Pallas kernels for 0%

commit v1 on v0

v1 whole, which is shorter than its diff:
```python
import functools

import jax
import jax.numpy as jnp
from jax import lax
from jax.experimental import pallas as pl
from jax.experimental.pallas import tpu as pltpu
from jax.sharding import PartitionSpec as P

HEADS = 4
HALF = 64
EPS = 1e-06
MASKED = -1e30
BF = jnp.bfloat16
F32 = jnp.float32
MESH = pl.DeviceIdType.MESH
NEAR = 4
VMEM_SPEC = pl.BlockSpec(memory_space=pltpu.VMEM)


def dot(a, b):
    return lax.dot_general(a, b, (((1,), (0,)), ((), ())), preferred_element_type=F32)


def dot_t(a, b):
    return lax.dot_general(a, b, (((1,), (1,)), ((), ())), preferred_element_type=F32)


def t_dot(a, b):
    return lax.dot_general(a, b, (((0,), (0,)), ((), ())), preferred_element_type=F32)


def head_mask(head, rows, width, dtype):
    lane = lax.broadcasted_iota(jnp.int32, (rows, width), 1)
    return (lane // (width // HEADS) == head).astype(dtype)


def unit(rows):
    inverse = lax.rsqrt(jnp.mean(rows * rows, axis=-1, keepdims=True) + EPS)
    return inverse, rows * inverse


def unit_backward(incoming, inverse, unit_rows, gain):
    scaled = incoming * gain
    mean = jnp.mean(scaled * unit_rows, axis=-1, keepdims=True)
    return inverse * (scaled - unit_rows * mean)


def greet(count, peer_of):
    barrier = pltpu.get_barrier_semaphore()

    def tell(k, carry):
        pl.semaphore_signal(barrier, inc=1, device_id=peer_of(k), device_id_type=MESH)
        return carry

    lax.fori_loop(1, count, tell, 0)
    return barrier


def send_all(count, me, device_of, source_of, target, sems):
    send_sem, recv_sem = sems

    def step(k, carry):
        p = lax.rem(me + k, count)
        pltpu.make_async_remote_copy(
            src_ref=source_of(p),
            dst_ref=target.at[me],
            send_sem=send_sem.at[p],
            recv_sem=recv_sem.at[me],
            device_id=device_of(p),
            device_id_type=MESH,
        ).start()
        return carry

    lax.fori_loop(1, count, step, 0)


def wait_all(count, me, device_of, source_of, target, sems):
    send_sem, recv_sem = sems

    def step(k, carry):
        p = lax.rem(me + k, count)
        copy = pltpu.make_async_remote_copy(
            src_ref=source_of(p),
            dst_ref=target.at[p],
            send_sem=send_sem.at[p],
            recv_sem=recv_sem.at[p],
            device_id=device_of(p),
            device_id_type=MESH,
        )
        copy.wait_recv()
        copy.wait_send()
        return carry

    lax.fori_loop(1, count, step, 0)


def dma_pair(count):
    return [pltpu.SemaphoreType.DMA((count,)), pltpu.SemaphoreType.DMA((count,))]


def comm_params(collective_id):
    return pltpu.CompilerParams(collective_id=collective_id, has_side_effects=True)


def freq_exchange_kernel(count, x_ref, out_ref, send_sem, recv_sem):
    me = lax.axis_index("freq")

    def device_of(p):
        return {"freq": p}

    barrier = greet(count, lambda k: device_of(lax.rem(me + k, count)))
    pl.semaphore_wait(barrier, count - 1)
    send_all(count, me, device_of, lambda p: x_ref.at[p], out_ref, (send_sem, recv_sem))
    out_ref[me] = x_ref[me]
    wait_all(count, me, device_of, lambda p: x_ref.at[p], out_ref, (send_sem, recv_sem))


def freq_exchange(x, collective_id):
    count = x.shape[0]
    return pl.pallas_call(
        functools.partial(freq_exchange_kernel, count),
        out_shape=jax.ShapeDtypeStruct(x.shape, x.dtype),
        in_specs=[VMEM_SPEC],
        out_specs=VMEM_SPEC,
        scratch_shapes=dma_pair(count),
        compiler_params=comm_params(collective_id),
        name=f"freq_exchange_{collective_id}",
    )(x)


def to_time_kernel(bins, halo, a_ref, b_ref, a_out, b_out, send_a, recv_a, send_b, recv_b):
    count = 2 * bins
    me = lax.axis_index("tm")
    mine = lax.div(me, bins)
    span = bins + halo

    def device_of(p):
        return {"tm": p}

    barrier = greet(count, lambda k: device_of(lax.rem(me + k, count)))
    pl.semaphore_wait(barrier, count - 1)
    arrays = ((a_ref, a_out, send_a, recv_a), (b_ref, b_out, send_b, recv_b))

    def copy_to(part, half, bin_id):
        src, dst, send, recv = part
        slot = me - halo * half
        return pltpu.make_async_remote_copy(
            src_ref=src.at[bin_id],
            dst_ref=dst.at[slot],
            send_sem=send.at[bin_id + bins * half],
            recv_sem=recv.at[slot],
            device_id=device_of(bin_id + bins * half),
            device_id_type=MESH,
        )

    def each_target(action):
        for half in range(2):
            needed = (me < span) if half == 0 else (me >= halo)

            @pl.when(needed)
            def _():
                def step(k, carry):
                    bin_id = lax.rem(me + k, bins)

                    @pl.when(bin_id + bins * half != me)
                    def _():
                        for part in arrays:
                            action(copy_to(part, half, bin_id))

                    return carry

                lax.fori_loop(0, bins, step, 0)

    each_target(lambda copy: copy.start())
    own_slot = me - halo * mine
    own_bin = me - bins * mine
    for src, dst, _, _ in arrays:
        dst[own_slot] = src[own_bin]

    def arrive(slot, carry):
        @pl.when(slot != own_slot)
        def _():
            for src, dst, send, recv in arrays:
                pltpu.make_async_remote_copy(
                    src_ref=src.at[own_bin],
                    dst_ref=dst.at[slot],
                    send_sem=send.at[me],
                    recv_sem=recv.at[slot],
                    device_id=device_of(slot + halo * mine),
                    device_id_type=MESH,
                ).wait_recv()

        return carry

    lax.fori_loop(0, span, arrive, 0)
    each_target(lambda copy: copy.wait_send())


def to_time(a, b, collective_id):
    bins = a.shape[0]
    halo = bins // 2
    shape = (bins + halo,) + a.shape[1:]
    return pl.pallas_call(
        functools.partial(to_time_kernel, bins, halo),
        out_shape=[jax.ShapeDtypeStruct(shape, a.dtype)] * 2,
        in_specs=[VMEM_SPEC] * 2,
        out_specs=[VMEM_SPEC] * 2,
        scratch_shapes=[
            pltpu.SemaphoreType.DMA((2 * bins,)),
            pltpu.SemaphoreType.DMA((bins + halo,)),
            pltpu.SemaphoreType.DMA((2 * bins,)),
            pltpu.SemaphoreType.DMA((bins + halo,)),
        ],
        compiler_params=comm_params(collective_id),
        name="to_time",
    )(a, b)


def from_time_kernel(bins, x_ref, out_ref, send_sem, recv_sem):
    index = lax.axis_index("tm")
    base = lax.div(index, bins) * bins
    me = index - base

    def device_of(p):
        return {"tm": base + p}

    barrier = greet(bins, lambda k: device_of(lax.rem(me + k, bins)))
    pl.semaphore_wait(barrier, bins - 1)
    send_all(bins, me, device_of, lambda p: x_ref.at[p], out_ref, (send_sem, recv_sem))
    out_ref[me] = x_ref[me]
    wait_all(bins, me, device_of, lambda p: x_ref.at[p], out_ref, (send_sem, recv_sem))


def from_time(x, collective_id):
    bins = x.shape[0]
    return pl.pallas_call(
        functools.partial(from_time_kernel, bins),
        out_shape=jax.ShapeDtypeStruct(x.shape, x.dtype),
        in_specs=[VMEM_SPEC],
        out_specs=VMEM_SPEC,
        scratch_shapes=dma_pair(bins),
        compiler_params=comm_params(collective_id),
        name="from_time",
    )(x)


def reduce_kernel(
    plane, near, far, w_ref, g_ref, out_ref, gain_ref,
    plane_in, near_src, near_in, far_src, far_in, back_src, back_in, last_src, last_in,
    gain_src, gain_plane, gain_near, gain_far, *sems
):
    tm, freq = lax.axis_index("tm"), lax.axis_index("freq")
    core, high = lax.rem(freq, 2), lax.div(freq, 2)
    low = lax.rem(tm, near)
    column = lax.div(tm, near)
    here = column * 2 + core

    def in_plane(p):
        return {"tm": lax.div(p, 2) * near + low, "freq": high * 2 + lax.rem(p, 2)}

    def in_near(p):
        return {"tm": column * near + p, "freq": freq}

    def in_far(p):
        return {"tm": tm, "freq": p * 2 + core}

    pairs = [(sems[2 * i], sems[2 * i + 1]) for i in range(len(sems) // 2)]
    barrier = greet(plane, lambda k: in_plane(lax.rem(here + k, plane)))
    greet(near, lambda k: in_near(lax.rem(low + k, near)))
    greet(far, lambda k: in_far(lax.rem(high + k, far)))
    pl.semaphore_wait(barrier, plane + near + far - 3)

    def both(count, me, device_of, source_of, target, sem, gsrc, gtarget, gsem):
        send_all(count, me, device_of, source_of, target, sem)
        send_all(count, me, device_of, lambda p: gsrc, gtarget, gsem)

    def waited(count, me, device_of, source_of, target, sem, gsrc, gtarget, gsem):
        wait_all(count, me, device_of, source_of, target, sem)
        wait_all(count, me, device_of, lambda p: gsrc, gtarget, gsem)

    def total(ref, count):
        return lax.fori_loop(
            1, count, lambda i, acc: acc + ref[i].astype(F32), ref[0].astype(F32)
        )

    first = (plane, here, in_plane, lambda p: w_ref.at[p], plane_in, pairs[0], g_ref, gain_plane, pairs[1])
    both(*first)
    plane_in[here] = w_ref[here]
    gain_plane[here] = g_ref[...]
    waited(*first)
    rows = near_src.shape[1]
    near_src[...] = total(plane_in, plane).reshape(near, rows, near_src.shape[2])
    gain_src[0] = total(gain_plane, plane)

    second = (near, low, in_near, lambda p: near_src.at[p], near_in, pairs[2], gain_src.at[0], gain_near, pairs[3])
    both(*second)
    near_in[low] = near_src[low]
    gain_near[low] = gain_src[0]
    waited(*second)
    far_src[...] = total(near_in, near)
    gain_src[1] = total(gain_near, near)

    third = (far, high, in_far, lambda p: far_src, far_in, pairs[4], gain_src.at[1], gain_far, pairs[5])
    both(*third)
    far_in[high] = far_src[...]
    gain_far[high] = gain_src[1]
    waited(*third)
    back_src[...] = total(far_in, far)
    gain_ref[...] = total(gain_far, far)

    send_all(near, low, in_near, lambda p: back_src, back_in, pairs[6])
    back_in[low] = back_src[...]
    wait_all(near, low, in_near, lambda p: back_src, back_in, pairs[6])
    last_src[...] = back_in[...].reshape(last_src.shape).astype(last_src.dtype)

    send_all(plane, here, in_plane, lambda p: last_src, last_in, pairs[7])
    last_in[here] = last_src[...]
    wait_all(plane, here, in_plane, lambda p: last_src, last_in, pairs[7])
    out_ref[...] = last_in[...].astype(F32)


def reduce_over_devices(w, g, collective_id):
    plane, rows, width = w.shape
    near, far = NEAR, lax.axis_size("freq") // 2
    part = rows // near
    gain = g.shape
    counts = [plane, plane, near, near, far, far, near, plane]
    return pl.pallas_call(
        functools.partial(reduce_kernel, plane, near, far),
        out_shape=[jax.ShapeDtypeStruct(w.shape, F32), jax.ShapeDtypeStruct(gain, F32)],
        in_specs=[VMEM_SPEC] * 2,
        out_specs=[VMEM_SPEC] * 2,
        scratch_shapes=[
            pltpu.VMEM((plane, rows, width), BF),
            pltpu.VMEM((near, part, width), F32),
            pltpu.VMEM((near, part, width), F32),
            pltpu.VMEM((part, width), F32),
            pltpu.VMEM((far, part, width), F32),
            pltpu.VMEM((part, width), F32),
            pltpu.VMEM((near, part, width), F32),
            pltpu.VMEM((rows, width), BF),
            pltpu.VMEM((plane, rows, width), BF),
            pltpu.VMEM((2,) + gain, F32),
            pltpu.VMEM((plane,) + gain, F32),
            pltpu.VMEM((near,) + gain, F32),
            pltpu.VMEM((far,) + gain, F32),
        ]
        + [sem for count in counts for sem in dma_pair(count)],
        compiler_params=comm_params(collective_id),
        name="reduce_over_devices",
    )(w, g)


def freq_forward_kernel(x_ref, w_ref, gain_ref, h_ref, q_ref, k_ref, v_ref, o_ref, p_ref):
    rows, width = x_ref.shape
    x = x_ref[...].astype(F32)
    _, unit_rows = unit(x)
    norm = (unit_rows * gain_ref[0:1, :]).astype(BF)
    scale = (width // HEADS) ** (-0.5)
    q_ref[...] = dot(norm, w_ref[0]).astype(BF)
    k_ref[...] = dot(norm, w_ref[1]).astype(BF)
    v_ref[...] = dot(norm, w_ref[2]).astype(BF)
    mixed = jnp.zeros((rows, width), F32)
    for head in range(HEADS):
        mask = head_mask(head, rows, width, BF)
        scores = dot_t(q_ref[...] * mask, k_ref[...]) * scale
        e = jnp.exp(scores - jnp.max(scores, axis=-1, keepdims=True))
        p = e * (1.0 / jnp.sum(e, axis=-1, keepdims=True))
        p_ref[head] = p
        mixed = mixed + dot(p.astype(BF), v_ref[...] * mask)
    o_ref[...] = mixed.astype(BF)
    h_ref[...] = (x + dot(o_ref[...], w_ref[3])).astype(BF)


def freq_backward_kernel(
    scale_out, x_ref, gh_ref, q_ref, k_ref, v_ref, o_ref, p_ref, w_ref, gain_ref, gi_ref, wg_ref, gg_ref
):
    rows, width = x_ref.shape
    scale = (width // HEADS) ** (-0.5)
    gain = gain_ref[0:1, :]
    inverse, unit_rows = unit(x_ref[...].astype(F32))
    norm = (unit_rows * gain).astype(BF)
    go = dot_t(gh_ref[...], w_ref[3]).astype(BF)
    gq = jnp.zeros((rows, width), F32)
    gk = jnp.zeros((rows, width), F32)
    gv = jnp.zeros((rows, width), F32)
    for head in range(HEADS):
        mask = head_mask(head, rows, width, BF)
        p = p_ref[head]
        go_head = go * mask
        dp = dot_t(go_head, v_ref[...])
        delta = jnp.sum(dp * p, axis=-1, keepdims=True)
        ds = (p * (dp - delta) * scale).astype(BF)
        gq = gq + dot(ds, k_ref[...] * mask)
        gk = gk + t_dot(ds, q_ref[...] * mask)
        gv = gv + t_dot(p.astype(BF), go_head)
    gq, gk, gv = gq.astype(BF), gk.astype(BF), gv.astype(BF)
    gn = dot_t(gq, w_ref[0]) + dot_t(gk, w_ref[1]) + dot_t(gv, w_ref[2])
    gi_ref[...] = (
        gh_ref[...].astype(F32) + unit_backward(gn, inverse, unit_rows, gain)
    ).astype(BF)
    gg_ref[...] = jnp.sum(gn * unit_rows, axis=0, keepdims=True) * scale_out
    wg_ref[0] = (t_dot(norm, gq) * scale_out).astype(BF)
    wg_ref[1] = (t_dot(norm, gk) * scale_out).astype(BF)
    wg_ref[2] = (t_dot(norm, gv) * scale_out).astype(BF)
    wg_ref[3] = (t_dot(o_ref[...], gh_ref[...]) * scale_out).astype(BF)


def time_kernel(
    scale_out, own, h_ref, up_ref, w_ref, gain_ref, gh_ref, wg_ref, gg_ref,
    n_s, q_s, k_s, v_s, go_s, o_s, gq_s, gk_s, gv_s, u_s
):
    blocks, sub, width = h_ref.shape
    rows = blocks * sub
    scale = (width // HEADS) ** (-0.5)
    gain = gain_ref[1:2, :]
    _, unit_rows = unit(h_ref[...].astype(F32).reshape(rows, width))
    n_s[...] = (unit_rows * gain).astype(BF)
    q_s[...] = dot(n_s[...], w_ref[4]).astype(BF)
    k_s[...] = dot(n_s[...], w_ref[5]).astype(BF)
    v_s[...] = dot(n_s[...], w_ref[6]).astype(BF)
    u_s[...] = up_ref[...].astype(F32).reshape(rows, width).astype(BF)
    go_s[...] = dot_t(u_s[...], w_ref[7]).astype(BF)
    gk_s[...] = jnp.zeros_like(gk_s)
    gv_s[...] = jnp.zeros_like(gv_s)

    queries, keys = 2 * HALF, 4 * HALF
    offset = lax.broadcasted_iota(jnp.int32, (queries, keys), 1) - lax.broadcasted_iota(
        jnp.int32, (queries, keys), 0
    )

    def block(i, carry):
        q_at = pl.ds(pl.multiple_of(i * queries, queries), queries)
        k_at = pl.ds(pl.multiple_of(i * HALF, HALF), keys)
        q, go, k, v = q_s[q_at, :], go_s[q_at, :], k_s[k_at, :], v_s[k_at, :]
        distance = offset - HALF * i
        allowed = (distance >= -HALF) & (distance < HALF)
        mixed = jnp.zeros((queries, width), F32)
        gq = jnp.zeros((queries, width), F32)
        gk = jnp.zeros((keys, width), F32)
        gv = jnp.zeros((keys, width), F32)
        for head in range(HEADS):
            mask = head_mask(head, queries, width, BF)
            key_mask = head_mask(head, keys, width, BF)
            q_head, go_head = q * mask, go * mask
            scores = jnp.where(allowed, dot_t(q_head, k) * scale, MASKED)
            e = jnp.exp(scores - jnp.max(scores, axis=-1, keepdims=True))
            p = e * (1.0 / jnp.sum(e, axis=-1, keepdims=True))
            p_half = p.astype(BF)
            mixed = mixed + dot(p_half, v * key_mask)
            dp = dot_t(go_head, v)
            delta = jnp.sum(dp * p, axis=-1, keepdims=True)
            ds = (p * (dp - delta) * scale).astype(BF)
            gq = gq + dot(ds, k * key_mask)
            gk = gk + t_dot(ds, q_head)
            gv = gv + t_dot(p_half, go_head)
        o_s[q_at, :] = mixed.astype(BF)
        gq_s[q_at, :] = gq.astype(BF)
        gk_s[k_at, :] += gk
        gv_s[k_at, :] += gv
        return carry

    lax.fori_loop(0, rows // queries, block, 0)

    half = lax.div(lax.axis_index("tm"), own // sub)
    first = pl.multiple_of(half * (own // 2), own // 2)
    at = pl.ds(first, own)
    gq, gk, gv = gq_s[at, :], gk_s[at, :].astype(BF), gv_s[at, :].astype(BF)
    gn = dot_t(gq, w_ref[4]) + dot_t(gk, w_ref[5]) + dot_t(gv, w_ref[6])
    own_blocks = pl.ds(lax.div(first, sub), own // sub)
    inverse, unit_own = unit(h_ref[own_blocks].astype(F32).reshape(own, width))
    upstream = u_s[at, :]
    gh = upstream.astype(F32) + unit_backward(gn, inverse, unit_own, gain)
    gh_ref[...] = gh.reshape(own // sub, sub, width).astype(BF)
    gg_ref[...] = jnp.sum(gn * unit_own, axis=0, keepdims=True) * scale_out
    norm = n_s[at, :]
    wg_ref[0] = (t_dot(norm, gq) * scale_out).astype(BF)
    wg_ref[1] = (t_dot(norm, gk) * scale_out).astype(BF)
    wg_ref[2] = (t_dot(norm, gv) * scale_out).astype(BF)
    wg_ref[3] = (t_dot(o_s[at, :], upstream) * scale_out).astype(BF)


def per_device(features, upstream, weights, gains):
    frames, bins, width = features.shape
    rows = bins * lax.axis_size("freq")
    frame_total = frames * lax.axis_size("tm")
    scale_out = (frame_total * rows) ** (-0.5)
    shape = jax.ShapeDtypeStruct

    x = freq_exchange(features, 0).reshape(rows, width)
    hidden, q, k, v, mixed, p = pl.pallas_call(
        freq_forward_kernel,
        out_shape=[shape((rows, width), BF)] * 5 + [shape((HEADS, rows, rows), F32)],
        name="freq_forward",
    )(x, weights, gains)
    back = freq_exchange(hidden.reshape(features.shape), 1)
    h_time, up_time = to_time(back.transpose(1, 0, 2), upstream.transpose(1, 0, 2), 2)
    blocks = h_time.shape[0]
    own = bins * frames
    all_rows = blocks * frames
    half_rows = pltpu.VMEM((all_rows, width), BF)
    full_rows = pltpu.VMEM((all_rows, width), F32)
    gh_time, time_grads, time_gain = pl.pallas_call(
        functools.partial(time_kernel, scale_out, own),
        out_shape=[
            shape((bins, frames, width), BF),
            shape((4, width, width), BF),
            shape((1, width), F32),
        ],
        scratch_shapes=[half_rows] * 7 + [full_rows] * 2 + [half_rows],
        name="time_attention",
    )(h_time, up_time, weights, gains)
    gh_local = from_time(gh_time, 3).transpose(1, 0, 2)
    gh = freq_exchange(gh_local, 4).reshape(rows, width)
    gi, freq_grads, freq_gain = pl.pallas_call(
        functools.partial(freq_backward_kernel, scale_out),
        out_shape=[
            shape((rows, width), BF),
            shape((4, width, width), BF),
            shape((1, width), F32),
        ],
        name="freq_backward",
    )(x, gh, q, k, v, mixed, p, weights, gains)
    grad_input = freq_exchange(gi.reshape(features.shape), 5)
    plane = lax.axis_size("tm") // NEAR * 2
    stacked = jnp.concatenate([freq_grads, time_grads], axis=0)
    gain_rows = jnp.concatenate([freq_gain, time_gain], axis=0).reshape(4, width // 2)
    gain_rows = jnp.pad(gain_rows, ((0, 4), (0, 0)))
    sums, gain_sums = reduce_over_devices(stacked.reshape(plane, -1, width), gain_rows, 6)
    return (
        grad_input,
        sums.reshape(8, width, width),
        gain_sums[:4].reshape(2, width),
    )


def solution(mesh):
    return jax.shard_map(
        per_device,
        mesh=mesh,
        in_specs=(P("tm", "freq", None), P("tm", "freq", None), P(), P()),
        out_specs=(P("tm", "freq", None), P(), P()),
        check_vma=False,
    )
```

time: 1130 us -> 204 us (0.18)
  waiting for transfers between devices: 481 us -> 0 us
  starting transfers between devices: 366 us -> 0 us
  Pallas kernels: 0 us -> 190 us
  blocking collectives: 154 us -> 0 us
  matrix products: 52.5 us -> 0 us
  local copies, waits for them, and re-layouts: 42.2 us -> 8.99 us
  other arithmetic: 19.1 us -> 2.81 us
  between operations: 16.3 us -> 0.71 us
    psum x1 -> x0, waiting for transfers between devices: 371 us -> none  [per_device(): lax.psum((jnp.concatenate([freq_stack, time_stack], axis=0), jnp.stack([g...]
    ppermute x96 -> x0, starting transfers between devices: 304 us -> none  [passed_along(): return lax.ppermute(block, axis, route)]
    pallas_call x0 -> x10, Pallas kernels: none -> 190 us  [the longest x4 81.8 us: freq_exchange(): pl.pallas_call(functools.partial(freq_exchange_kernel, count), out_shape=...]
    psum x1 -> x0, blocking collectives: 115 us -> none  [per_device(): lax.psum((jnp.concatenate([freq_stack, time_stack], axis=0), jnp.stack([g...]
    all_to_all x7 -> x0, starting transfers between devices: 61.4 us -> none  [the longest x1 15.4 us: per_device(): lax.all_to_all(key_one, 'freq', split_axis=0, concat_axis=1, tiled=True)]
    all_to_all x7 -> x0, waiting for transfers between devices: 57.9 us -> none  [the longest x1 15.2 us: per_device(): lax.all_to_all(value_one, 'freq', split_axis=0, concat_axis=1, tiled=True)]
    ppermute x96 -> x0, waiting for transfers between devices: 51.6 us -> none  [passed_along(): return lax.ppermute(block, axis, route)]
    dot_general x34 -> x0, matrix products: 44.2 us -> none  [the longest x8 8.8 us: project_back(): lax.dot_general(flat_rows, matrix, (((1,), (1,)), ((), ())), preferred_el...]
  transfers between devices with their start and end apart: 104 -> 0, of which waited for: 21 -> 0; matrix products, arithmetic and copies ran while one was open for 6% -> 0% of each run, Pallas kernels for 0% -> 0%
where the time goes in v1:
time: 204 us; the launch traced here: 203 us
  Pallas kernels  190 us (93%)
  local copies, waits for them, and re-layouts  8.99 us (4%)
  other arithmetic  2.81 us (1%)
    pallas_call x4, Pallas kernels, freq_exchange(): pl.pallas_call(functools.partial(freq_exchange_kernel, count), out_shape=...  81.8 us
    pallas_call x1, Pallas kernels, reduce_over_devices(): pl.pallas_call(functools.partial(reduce_kernel, plane, near, far), out_sh...  58.2 us
    pallas_call x1, Pallas kernels, to_time(): pl.pallas_call(functools.partial(to_time_kernel, bins, halo), out_shape=[...  20.9 us
    pallas_call x1, Pallas kernels, from_time(): pl.pallas_call(functools.partial(from_time_kernel, bins), out_shape=jax.S...  12.6 us
    pallas_call x1, Pallas kernels, per_device(): pl.pallas_call(functools.partial(time_kernel, scale_out, own), out_shape=...  8.94 us
    pallas_call x1, Pallas kernels, per_device(): pl.pallas_call(functools.partial(freq_backward_kernel, scale_out), out_sh...  4.6 us

profile of v1, /device:TPU:1, one launch (start us, length us, event | category | flops | bytes accessed | tf_op | source)
XLA Modules:
  0.0 202.8 jit_solution(8391066649053232195)
XLA Ops:
  0.6 23.9 %freq_exchange_0.1 = bf16[8,32,256]{2,1,0:T(8,128)(2,1)} custom-call(bf16[8,32,256]{2,1,0:T(8,128)(2,1)} %x_ref.1), custom_call_target="tpu_custom_call" | custom-call | tf_op jit(solution)/shard_map/freq_exchange_0/pallas_call | solution.py:121
  24.5 3.4 %freq_forward.1 = (bf16[256,256]{1,0:T(8,128)(2,1)}, bf16[256,256]{1,0:T(8,128)(2,1)}, bf16[256,256]{1,0:T(8,128)(2,1)}, bf16[256,256]{1,0:T(8,128)(2,1)}, bf16[...) custom-call(bf16[256,256]{1,0:T(8,128)(2,1)} %bitcast.15, bf16[8,256,256]{2,1,0:T(8,128)(2,1)} %w_ref.5, f32[2,256]{1,0:T(2,128)} %gain_ref.5), custom_call_target="tpu_custom_call" | custom-call | tf_op jit(solution)/shard_map/freq_forward/pallas_call | solution.py:492
  27.9 17.3 %freq_exchange_1.1 = bf16[8,32,256]{2,1,0:T(8,128)(2,1)} custom-call(bf16[8,32,256]{2,1,0:T(8,128)(2,1)} %bitcast.20), custom_call_target="tpu_custom_call" | custom-call | tf_op jit(solution)/shard_map/freq_exchange_1/pallas_call | solution.py:121
  45.2 1.8 copy_bitcast_fusion.1
  47.1 20.9 %to_time.1 = (bf16[48,8,256]{2,1,0:T(8,128)(2,1)}, bf16[48,8,256]{2,1,0:T(8,128)(2,1)}) custom-call(bf16[32,8,256]{2,1,0:T(8,128)(2,1)} %get-tuple-element.36.a_ref, bf16[32,8,256]{2,1,0:T(8,128)(2,1)} %get-tuple-element.35.b_ref), custom_call_target="tpu_custom_call" | custom-call | tf_op jit(solution)/shard_map/to_time/pallas_call | solution.py:204
  67.9 8.9 %time_attention.1 = (bf16[32,8,256]{2,1,0:T(8,128)(2,1)}, bf16[4,256,256]{2,1,0:T(8,128)(2,1)}, f32[1,256]{1,0:T(1,128)}) custom-call(bf16[48,8,256]{2,1,0:T(8,128)(2,1)} %get-tuple-element.20.h_ref, bf16[48,8,256]{2,1,0:T(8,128)(2,1)} %get-tuple-element.21.up_ref, bf16[8,256,256]{2,1,0:T(8,128)(2,1)} %w_ref.5, f32[2,256]{1,0:T(2,128)} %gain_ref.5), custom_call_target="tpu_custom_call" | custom-call | tf_op jit(solution)/shard_map/time_attention/pallas_call | solution.py:504
  76.9 0.0 copy-start.2
  76.9 0.0 copy-start.1
  76.9 12.6 %from_time.1 = bf16[32,8,256]{2,1,0:T(8,128)(2,1)} custom-call(bf16[32,8,256]{2,1,0:T(8,128)(2,1)} %get-tuple-element.22.x_ref), custom_call_target="tpu_custom_call" | custom-call | tf_op jit(solution)/shard_map/from_time/pallas_call | solution.py:237
  89.5 1.6 copy.13
  91.1 21.2 %freq_exchange_4.1 = bf16[8,32,256]{2,1,0:T(8,128)(2,1)} custom-call(bf16[8,32,256]{2,1,0:T(8,128)(2,1)} %bitcast.18), custom_call_target="tpu_custom_call" | custom-call | tf_op jit(solution)/shard_map/freq_exchange_4/pallas_call | solution.py:121
  112.3 4.6 %freq_backward.1 = (bf16[256,256]{1,0:T(8,128)(2,1)}, bf16[4,256,256]{2,1,0:T(8,128)(2,1)}, f32[1,256]{1,0:T(1,128)}) custom-call(bf16[256,256]{1,0:T(8,128)(2,1)} %bitcast.16, bf16[256,256]{1,0:T(8,128)(2,1)} %bitcast.17, bf16[256,256]{1,0:T(8,128)(2,1)} %get-tuple-element.23.q_ref, bf16[256,256]{1,0:T(8,128)(2,1)} %get-tuple-element.24.k_ref, ...), custom_call_target="tpu_custom_call" | custom-call | tf_op jit(solution)/shard_map/freq_backward/pallas_call | solution.py:516
  116.9 19.3 %freq_exchange_5.1 = bf16[8,32,256]{2,1,0:T(8,128)(2,1)} custom-call(bf16[8,32,256]{2,1,0:T(8,128)(2,1)} %bitcast.19), custom_call_target="tpu_custom_call" | custom-call | tf_op jit(solution)/shard_map/freq_exchange_5/pallas_call | solution.py:121
  136.2 0.0 copy-done.2
  136.2 0.0 copy-start
  136.2 0.7 pad_maximum_fusion.1
  137.0 0.6 pad.4.g_ref
  137.6 0.0 copy-done.1
  137.6 2.1 %pad_maximum_fusion = bf16[8,256,256]{2,1,0:T(8,128)(2,1)} fusion(bf16[4,256,256]{2,1,0:T(8,128)(2,1)S(1)} %copy-done.1, bf16[4,256,256]{2,1,0:T(8,128)(2,1)} %get-tuple-element.29), kind=kLoop, calls=%fused_computation | loop fusion | flops 524288 | bytes 2097152 | tf_op jit(solution)/shard_map/concatenate | solution.py:527
  139.7 58.2 %reduce_over_devices.1 = (f32[32,64,256]{2,1,0:T(8,128)}, f32[8,128]{1,0:T(8,128)}) custom-call(bf16[32,64,256]{2,1,0:T(8,128)(2,1)} %bitcast.13, f32[8,128]{1,0:T(8,128)} %pad.4.g_ref), custom_call_target="tpu_custom_call" | custom-call | tf_op jit(solution)/shard_map/reduce_over_devices/pallas_call | solution.py:329
  197.9 0.7 slice.3
  198.6 0.6 reshape.37
  199.1 0.0 copy-done
  199.1 0.7 copy.16
  199.8 3.0 %copy.17 = f32[8,256,256]{2,1,0:T(8,128)} copy(f32[8,256,256]{2,1,0:T(8,128)} %bitcast.14) | data formatting | bytes 4194304
  (1 shorter events, 0.0 us)
Async XLA Ops:
  76.9 59.4 %copy-start.2 = (f32[1,256]{1,0:T(1,128)S(1)}, f32[1,256]{1,0:T(1,128)}, u32[]{:S(2)}) copy-start(f32[1,256]{1,0:T(1,128)} %get-tuple-element.32) | copy-start | bytes 3076
  76.9 60.7 %copy-start.1 = (bf16[4,256,256]{2,1,0:T(8,128)(2,1)S(1)}, bf16[4,256,256]{2,1,0:T(8,128)(2,1)}, u32[]{:S(2)}) copy-start(bf16[4,256,256]{2,1,0:T(8,128)(2,1)} %get-tuple-element.30) | copy-start | bytes 1572868
  136.2 62.9 %copy-start = (bf16[8,32,256]{2,1,0:T(8,128)(2,1)S(1)}, bf16[8,32,256]{2,1,0:T(8,128)(2,1)}, u32[]{:S(2)}) copy-start(bf16[8,32,256]{2,1,0:T(8,128)(2,1)} %freq_exchange_5.1) | copy-start | bytes 393220

commit v2 on v0

v2 whole, which is shorter than its diff:
```python
import functools

import jax
import jax.numpy as jnp
from jax import lax
from jax.experimental import pallas as pl
from jax.experimental.pallas import tpu as pltpu
from jax.sharding import PartitionSpec as P

HEADS = 4
HALF = 64
EPS = 1e-06
MASKED = -1e30
BF = jnp.bfloat16
F32 = jnp.float32
MESH = pl.DeviceIdType.MESH
NEAR = 4
VMEM_SPEC = pl.BlockSpec(memory_space=pltpu.VMEM)


def dot(a, b):
    return lax.dot_general(a, b, (((1,), (0,)), ((), ())), preferred_element_type=F32)


def dot_t(a, b):
    return lax.dot_general(a, b, (((1,), (1,)), ((), ())), preferred_element_type=F32)


def t_dot(a, b):
    return lax.dot_general(a, b, (((0,), (0,)), ((), ())), preferred_element_type=F32)


def head_mask(head, rows, width, dtype):
    lane = lax.broadcasted_iota(jnp.int32, (rows, width), 1)
    return (lane // (width // HEADS) == head).astype(dtype)


def unit(rows):
    inverse = lax.rsqrt(jnp.mean(rows * rows, axis=-1, keepdims=True) + EPS)
    return inverse, rows * inverse


def unit_backward(incoming, inverse, unit_rows, gain):
    scaled = incoming * gain
    mean = jnp.mean(scaled * unit_rows, axis=-1, keepdims=True)
    return inverse * (scaled - unit_rows * mean)


class Exchange:
    def __init__(self, count, me, device_of, source_of, target, sems):
        self.count, self.me, self.device_of = count, me, device_of
        self.source_of, self.target, self.sems = source_of, target, sems

    def copy(self, p, slot):
        send_sem, recv_sem = self.sems
        return pltpu.make_async_remote_copy(
            src_ref=self.source_of(p),
            dst_ref=self.target.at[slot],
            send_sem=send_sem.at[p],
            recv_sem=recv_sem.at[slot],
            device_id=self.device_of(p),
            device_id_type=MESH,
        )

    def others(self, action):
        def step(k, carry):
            action(lax.rem(self.me + k, self.count))
            return carry

        lax.fori_loop(1, self.count, step, 0)

    def start(self):
        self.others(lambda p: self.copy(p, self.me).start())
        self.target[self.me] = self.source_of(self.me)[...]

    def wait(self):
        def step(p):
            copy = self.copy(p, p)
            copy.wait_recv()
            copy.wait_send()

        self.others(step)


class ToTime:
    def __init__(self, bins, me, source, target, sems):
        self.bins, self.halo, self.me = bins, bins // 2, me
        self.mine = lax.div(me, bins)
        self.source, self.target, self.sems = source, target, sems

    def copy(self, bin_id, half, slot):
        send_sem, recv_sem = self.sems
        return pltpu.make_async_remote_copy(
            src_ref=self.source.at[bin_id],
            dst_ref=self.target.at[slot],
            send_sem=send_sem.at[bin_id + self.bins * half],
            recv_sem=recv_sem.at[slot],
            device_id={"tm": bin_id + self.bins * half},
            device_id_type=MESH,
        )

    def each_target(self, action):
        for half in range(2):
            needed = (self.me < self.bins + self.halo) if half == 0 else (self.me >= self.halo)

            @pl.when(needed)
            def _():
                def step(k, carry):
                    bin_id = lax.rem(self.me + k, self.bins)

                    @pl.when(bin_id + self.bins * half != self.me)
                    def _():
                        action(self.copy(bin_id, half, self.me - self.halo * half))

                    return carry

                lax.fori_loop(0, self.bins, step, 0)

    def start(self):
        self.each_target(lambda copy: copy.start())
        own = self.me - self.halo * self.mine
        self.target[own] = self.source[self.me - self.bins * self.mine]

    def wait(self):
        own = self.me - self.halo * self.mine
        send_sem, recv_sem = self.sems

        def arrive(slot, carry):
            @pl.when(slot != own)
            def _():
                pltpu.make_async_remote_copy(
                    src_ref=self.source.at[0],
                    dst_ref=self.target.at[slot],
                    send_sem=send_sem.at[0],
                    recv_sem=recv_sem.at[slot],
                    device_id={"tm": slot + self.halo * self.mine},
                    device_id_type=MESH,
                ).wait_recv()

            return carry

        lax.fori_loop(0, self.bins + self.halo, arrive, 0)
        self.each_target(lambda copy: copy.wait_send())


def total(ref, count):
    return lax.fori_loop(1, count, lambda i, acc: acc + ref[i].astype(F32), ref[0].astype(F32))


def swapped(value):
    return jnp.swapaxes(value.astype(F32), 0, 1).astype(BF)


def layer_kernel(scale_out, names, x_ref, up_ref, w_ref, gain_ref, gi_ref, sum_ref, gain_out, *scratch):
    s = dict(zip(names, scratch))
    frames, bins, width = x_ref.shape
    scale = (width // HEADS) ** (-0.5)
    tm, freq = lax.axis_index("tm"), lax.axis_index("freq")
    tm_count, freq_count = s["rs_time_in"].shape[0] // 2 * NEAR, frames
    core, high = lax.rem(freq, 2), lax.div(freq, 2)
    low, column = lax.rem(tm, NEAR), lax.div(tm, NEAR)
    here = column * 2 + core
    plane, far = s["rs_time_in"].shape[0], freq_count // 2
    rows = bins * freq_count
    base = lax.div(tm, bins) * bins

    def in_freq(p):
        return {"freq": p}

    def in_tm(p):
        return {"tm": p}

    def in_half(p):
        return {"tm": base + p}

    def in_plane(p):
        return {"tm": lax.div(p, 2) * NEAR + low, "freq": high * 2 + lax.rem(p, 2)}

    def in_near(p):
        return {"tm": column * NEAR + p, "freq": freq}

    def in_far(p):
        return {"tm": tm, "freq": p * 2 + core}

    def sems(name):
        return s[name + "_send"], s[name + "_recv"]

    barrier = pltpu.get_barrier_semaphore()

    def tell(first, last, peer_of):
        def step(k, carry):
            pl.semaphore_signal(barrier, inc=1, device_id=peer_of(k), device_id_type=MESH)
            return carry

        lax.fori_loop(first, last, step, 0)

    tell(1, freq_count, lambda k: in_freq(lax.rem(freq + k, freq_count)))
    tell(0, plane // 2, lambda k: in_plane(lax.rem(column + k, plane // 2) * 2 + 1 - core))
    tell(1, tm_count, lambda k: in_tm(lax.rem(tm + k, tm_count)))
    s["up_t"][...] = swapped(up_ref[...])
    pl.semaphore_wait(barrier, freq_count - 1 + plane // 2 + tm_count - 1)

    to_frames = Exchange(freq_count, freq, in_freq, lambda p: x_ref.at[p], s["x_f"], sems("x"))
    to_frames.start()
    up_time = ToTime(bins, tm, s["up_t"], s["up_w"], sems("up"))
    up_time.start()
    to_frames.wait()

    gain = gain_ref[0:1, :]
    x = s["x_f"][...].astype(F32).reshape(rows, width)
    _, unit_rows = unit(x)
    norm = (unit_rows * gain).astype(BF)
    s["n1"][...] = norm
    s["q1"][...] = dot(norm, w_ref[0]).astype(BF)
    s["k1"][...] = dot(norm, w_ref[1]).astype(BF)
    s["v1"][...] = dot(norm, w_ref[2]).astype(BF)
    mixed = jnp.zeros((rows, width), F32)
    for head in range(HEADS):
        mask = head_mask(head, rows, width, BF)
        scores = dot_t(s["q1"][...] * mask, s["k1"][...]) * scale
        e = jnp.exp(scores - jnp.max(scores, axis=-1, keepdims=True))
        p = e * (1.0 / jnp.sum(e, axis=-1, keepdims=True))
        s["p1"][head] = p
        mixed = mixed + dot(p.astype(BF), s["v1"][...] * mask)
    s["o1"][...] = mixed.astype(BF)
    hidden = x + dot(s["o1"][...], w_ref[3])
    s["h_f"][...] = hidden.reshape(x_ref.shape).astype(BF)
    h_back = Exchange(freq_count, freq, in_freq, lambda p: s["h_f"].at[p], s["h_l"], sems("h"))
    h_back.start()

    up_time.wait()
    blocks, sub = s["up_w"].shape[:2]
    all_rows, own = blocks * sub, bins * sub
    s["up"][...] = s["up_w"][...].astype(F32).reshape(all_rows, width).astype(BF)
    s["go2"][...] = dot_t(s["up"][...], w_ref[7]).astype(BF)
    s["gk2"][...] = jnp.zeros_like(s["gk2"])
    s["gv2"][...] = jnp.zeros_like(s["gv2"])
    h_back.wait()
    s["h_t"][...] = swapped(s["h_l"][...])
    h_time = ToTime(bins, tm, s["h_t"], s["h_w"], sems("hw"))
    h_time.start()
    h_time.wait()

    gain = gain_ref[1:2, :]
    _, unit_rows = unit(s["h_w"][...].astype(F32).reshape(all_rows, width))
    norm = (unit_rows * gain).astype(BF)
    s["n2"][...] = norm
    s["q2"][...] = dot(norm, w_ref[4]).astype(BF)
    s["k2"][...] = dot(norm, w_ref[5]).astype(BF)
    s["v2"][...] = dot(norm, w_ref[6]).astype(BF)
    queries, keys = 2 * HALF, 4 * HALF
    offset = lax.broadcasted_iota(jnp.int32, (queries, keys), 1) - lax.broadcasted_iota(
        jnp.int32, (queries, keys), 0
    )

    def block(i, carry):
        q_at = pl.ds(pl.multiple_of(i * queries, queries), queries)
        k_at = pl.ds(pl.multiple_of(i * HALF, HALF), keys)
        q, go, k, v = s["q2"][q_at, :], s["go2"][q_at, :], s["k2"][k_at, :], s["v2"][k_at, :]
        distance = offset - HALF * i
        allowed = (distance >= -HALF) & (distance < HALF)
        mixed = jnp.zeros((queries, width), F32)
        gq = jnp.zeros((queries, width), F32)
        gk = jnp.zeros((keys, width), F32)
        gv = jnp.zeros((keys, width), F32)
        for head in range(HEADS):
            mask = head_mask(head, queries, width, BF)
            key_mask = head_mask(head, keys, width, BF)
            q_head, go_head = q * mask, go * mask
            scores = jnp.where(allowed, dot_t(q_head, k) * scale, MASKED)
            e = jnp.exp(scores - jnp.max(scores, axis=-1, keepdims=True))
            p = e * (1.0 / jnp.sum(e, axis=-1, keepdims=True))
            p_half = p.astype(BF)
            mixed = mixed + dot(p_half, v * key_mask)
            dp = dot_t(go_head, v)
            delta = jnp.sum(dp * p, axis=-1, keepdims=True)
            ds = (p * (dp - delta) * scale).astype(BF)
            gq = gq + dot(ds, k * key_mask)
            gk = gk + t_dot(ds, q_head)
            gv = gv + t_dot(p_half, go_head)
        s["o2"][q_at, :] = mixed.astype(BF)
        s["gq2"][q_at, :] = gq.astype(BF)
        s["gk2"][k_at, :] += gk
        s["gv2"][k_at, :] += gv
        return carry

    lax.fori_loop(0, all_rows // queries, block, 0)

    half = lax.div(tm, bins)
    first = pl.multiple_of(half * (own // 2), own // 2)
    at = pl.ds(first, own)
    gq, gk, gv = s["gq2"][at, :], s["gk2"][at, :].astype(BF), s["gv2"][at, :].astype(BF)
    gn = dot_t(gq, w_ref[4]) + dot_t(gk, w_ref[5]) + dot_t(gv, w_ref[6])
    own_blocks = pl.ds(half * (bins // 2), bins)
    inverse, unit_own = unit(s["h_w"][own_blocks].astype(F32).reshape(own, width))
    upstream = s["up"][at, :]
    gh = upstream.astype(F32) + unit_backward(gn, inverse, unit_own, gain)
    s["gh_t"][...] = gh.reshape(bins, sub, width).astype(BF)
    gh_back = Exchange(bins, tm - base, in_half, lambda p: s["gh_t"].at[p], s["gh_b"], sems("ghb"))
    gh_back.start()

    def place(name, index, value):
        per = width // s[name].shape[1]
        s[name][pl.ds(index * per, per)] = (
            (value * scale_out).reshape(per, s[name].shape[1], width).astype(BF)
        )

    def reduction(name):
        def stage(short, count, me, device_of, source_of, target):
            full = name + "_" + short
            return Exchange(count, me, device_of, source_of, s[target], sems(full))

        stack, result = s["wg_" + name], sum_ref.at[0 if name == "freq" else 1]
        return [
            stage("rs", plane, here, in_plane, lambda p: stack.at[p], "rs_" + name + "_in"),
            stage("near", NEAR, low, in_near, lambda p: s["near_" + name].at[p], "near_" + name + "_in"),
            stage("far", far, high, in_far, lambda p: s["far_" + name], "far_" + name + "_in"),
            stage("back", NEAR, low, in_near, lambda p: s["back_" + name], "back_" + name + "_in"),
            Exchange(plane, here, in_plane, lambda p: s["last_" + name], result, sems(name + "_last")),
        ]

    def after_plane(name):
        near = s["near_" + name]
        near[...] = total(s["rs_" + name + "_in"], plane).reshape(near.shape)

    def after_near(name):
        s["far_" + name][...] = total(s["near_" + name + "_in"], NEAR)

    def after_far(name):
        s["back_" + name][...] = total(s["far_" + name + "_in"], far)

    def after_back(name):
        last = s["last_" + name]
        last[...] = s["back_" + name + "_in"][...].reshape(last.shape).astype(BF)

    norm = s["n2"][at, :]
    place("wg_time", 0, t_dot(norm, gq))
    place("wg_time", 1, t_dot(norm, gk))
    place("wg_time", 2, t_dot(norm, gv))
    place("wg_time", 3, t_dot(s["o2"][at, :], upstream))
    time_gain = jnp.sum(gn * unit_own, axis=0, keepdims=True) * scale_out
    t_rs, t_near, t_far, t_back, t_last = reduction("time")
    t_rs.start()
    gh_back.wait()
    s["gh_l"][...] = swapped(s["gh_b"][...])
    gh_frames = Exchange(freq_count, freq, in_freq, lambda p: s["gh_l"].at[p], s["gh_f"], sems("gh"))
    gh_frames.start()
    t_rs.wait()
    after_plane("time")
    t_near.start()
    gh_frames.wait()

    gain = gain_ref[0:1, :]
    inverse, unit_rows = unit(s["x_f"][...].astype(F32).reshape(rows, width))
    gh32 = s["gh_f"][...].astype(F32).reshape(rows, width)
    gh = gh32.astype(BF)
    go = dot_t(gh, w_ref[3]).astype(BF)
    gq = jnp.zeros((rows, width), F32)
    gk = jnp.zeros((rows, width), F32)
    gv = jnp.zeros((rows, width), F32)
    for head in range(HEADS):
        mask = head_mask(head, rows, width, BF)
        p = s["p1"][head]
        go_head = go * mask
        dp = dot_t(go_head, s["v1"][...])
        delta = jnp.sum(dp * p, axis=-1, keepdims=True)
        ds = (p * (dp - delta) * scale).astype(BF)
        gq = gq + dot(ds, s["k1"][...] * mask)
        gk = gk + t_dot(ds, s["q1"][...] * mask)
        gv = gv + t_dot(p.astype(BF), go_head)
    gq, gk, gv = gq.astype(BF), gk.astype(BF), gv.astype(BF)
    gn = dot_t(gq, w_ref[0]) + dot_t(gk, w_ref[1]) + dot_t(gv, w_ref[2])
    gi = gh32 + unit_backward(gn, inverse, unit_rows, gain)
    s["gi_f"][...] = gi.reshape(x_ref.shape).astype(BF)
    gi_back = Exchange(freq_count, freq, in_freq, lambda p: s["gi_f"].at[p], gi_ref, sems("gi"))
    gi_back.start()
    norm = s["n1"][...]
    place("wg_freq", 0, t_dot(norm, gq))
    place("wg_freq", 1, t_dot(norm, gk))
    place("wg_freq", 2, t_dot(norm, gv))
    place("wg_freq", 3, t_dot(s["o1"][...], gh))
    f_rs, f_near, f_far, f_back, f_last = reduction("freq")
    f_rs.start()

    freq_gain = jnp.sum(gn * unit_rows, axis=0, keepdims=True) * scale_out
    s["g_0"][...] = jnp.concatenate([freq_gain, time_gain], axis=0)

    def gain_stage(number, count, me, device_of):
        source = s[f"g_{number}"]
        return Exchange(count, me, device_of, lambda p: source, s[f"g_in_{number}"], sems(f"g{number}"))

    g_plane = gain_stage(0, plane, here, in_plane)
    g_near = gain_stage(1, NEAR, low, in_near)
    g_far = gain_stage(2, far, high, in_far)
    g_plane.start()

    t_near.wait()
    after_near("time")
    t_far.start()
    f_rs.wait()
    after_plane("freq")
    f_near.start()
    g_plane.wait()
    s["g_1"][...] = total(s["g_in_0"], plane)
    g_near.start()
    t_far.wait()
    after_far("time")
    t_back.start()
    f_near.wait()
    after_near("freq")
    f_far.start()
    g_near.wait()
    s["g_2"][...] = total(s["g_in_1"], NEAR)
    g_far.start()
    t_back.wait()
    after_back("time")
    t_last.start()
    f_far.wait()
    after_far("freq")
    f_back.start()
    g_far.wait()
    gain_out[...] = total(s["g_in_2"], far)
    f_back.wait()
    after_back("freq")
    f_last.start()
    gi_back.wait()
    t_last.wait()
    f_last.wait()


def per_device(features, upstream, weights, gains):
    frames, bins, width = features.shape
    freq_count, tm_count = lax.axis_size("freq"), lax.axis_size("tm")
    rows = bins * freq_count
    scale_out = (frames * tm_count * rows) ** (-0.5)
    shape = jax.ShapeDtypeStruct
    plane, far = tm_count // NEAR * 2, freq_count // 2
    chunk = 4 * width // plane
    piece = chunk // NEAR
    span = bins + bins // 2
    all_rows = span * frames

    local = ((frames, bins, width), BF)
    turned = ((bins, frames, width), BF)
    window = ((span, frames, width), BF)
    flat = ((rows, width), BF)
    tall = ((all_rows, width), BF)
    buffers = dict(
        up_t=turned, up_w=window, x_f=local, n1=flat, q1=flat, k1=flat, v1=flat, o1=flat,
        p1=((HEADS, rows, rows), F32), h_f=local, h_l=local, h_t=turned, h_w=window,
        up=tall, go2=tall, n2=tall, q2=tall, k2=tall, v2=tall, o2=tall, gq2=tall,
        gk2=((all_rows, width), F32), gv2=((all_rows, width), F32),
        gh_t=turned, gh_b=turned, gh_l=local, gh_f=local, gi_f=local,
    )
    counts = dict(x=freq_count, h=freq_count, ghb=bins, gh=freq_count, gi=freq_count)
    for name in ("freq", "time"):
        buffers["wg_" + name] = ((plane, chunk, width), BF)
        buffers["rs_" + name + "_in"] = ((plane, chunk, width), BF)
        buffers["near_" + name] = ((NEAR, piece, width), F32)
        buffers["near_" + name + "_in"] = ((NEAR, piece, width), F32)
        buffers["far_" + name] = ((piece, width), F32)
        buffers["far_" + name + "_in"] = ((far, piece, width), F32)
        buffers["back_" + name] = ((piece, width), F32)
        buffers["back_" + name + "_in"] = ((NEAR, piece, width), F32)
        buffers["last_" + name] = ((chunk, width), BF)
        for stage, count in zip(("rs", "near", "far", "back", "last"), (plane, NEAR, far, NEAR, plane)):
            counts[name + "_" + stage] = count
    for number, count in enumerate((plane, NEAR, far)):
        buffers[f"g_{number}"] = ((2, width), F32)
        buffers[f"g_in_{number}"] = ((count, 2, width), F32)
        counts[f"g{number}"] = count
    names = list(buffers)
    scratch = [pltpu.VMEM(*buffers[name]) for name in names]
    for name, count in counts.items():
        for end in ("_send", "_recv"):
            names.append(name + end)
            scratch.append(pltpu.SemaphoreType.DMA((count,)))
    for name in ("up", "hw"):
        for end, count in (("_send", tm_count), ("_recv", span)):
            names.append(name + end)
            scratch.append(pltpu.SemaphoreType.DMA((count,)))

    grad_input, sums, gain_sums = pl.pallas_call(
        functools.partial(layer_kernel, scale_out, names),
        out_shape=[
            shape(features.shape, BF),
            shape((2, plane, chunk, width), BF),
            shape((2, width), F32),
        ],
        in_specs=[VMEM_SPEC] * 4,
        out_specs=[VMEM_SPEC] * 3,
        scratch_shapes=scratch,
        compiler_params=pltpu.CompilerParams(collective_id=0, has_side_effects=True),
        name="layer",
    )(features, upstream, weights, gains)
    return grad_input, sums.reshape(8, width, width).astype(F32), gain_sums


def solution(mesh):
    return jax.shard_map(
        per_device,
        mesh=mesh,
        in_specs=(P("tm", "freq", None), P("tm", "freq", None), P(), P()),
        out_specs=(P("tm", "freq", None), P(), P()),
        check_vma=False,
    )
```

time: 1130 us -> 117 us (0.10)
  waiting for transfers between devices: 481 us -> 0 us
  starting transfers between devices: 366 us -> 0 us
  blocking collectives: 154 us -> 0 us
  Pallas kernels: 0 us -> 112 us
  matrix products: 52.5 us -> 0 us
  local copies, waits for them, and re-layouts: 42.2 us -> 1.24 us
  other arithmetic: 19.1 us -> 2.77 us
  between operations: 16.3 us -> 0.66 us
    psum x1 -> x0, waiting for transfers between devices: 371 us -> none  [per_device(): lax.psum((jnp.concatenate([freq_stack, time_stack], axis=0), jnp.stack([g...]
    ppermute x96 -> x0, starting transfers between devices: 304 us -> none  [passed_along(): return lax.ppermute(block, axis, route)]
    psum x1 -> x0, blocking collectives: 115 us -> none  [per_device(): lax.psum((jnp.concatenate([freq_stack, time_stack], axis=0), jnp.stack([g...]
    pallas_call x0 -> x1, Pallas kernels: none -> 112 us  [per_device(): pl.pallas_call(functools.partial(layer_kernel, scale_out, names), out_sha...]
    all_to_all x7 -> x0, starting transfers between devices: 61.4 us -> none  [the longest x1 15.4 us: per_device(): lax.all_to_all(key_one, 'freq', split_axis=0, concat_axis=1, tiled=True)]
    all_to_all x7 -> x0, waiting for transfers between devices: 57.9 us -> none  [the longest x1 15.2 us: per_device(): lax.all_to_all(value_one, 'freq', split_axis=0, concat_axis=1, tiled=True)]
    ppermute x96 -> x0, waiting for transfers between devices: 51.6 us -> none  [passed_along(): return lax.ppermute(block, axis, route)]
    dot_general x34 -> x0, matrix products: 44.2 us -> none  [the longest x8 8.8 us: project_back(): lax.dot_general(flat_rows, matrix, (((1,), (1,)), ((), ())), preferred_el...]
  transfers between devices with their start and end apart: 104 -> 0, of which waited for: 21 -> 0; matrix products, arithmetic and copies ran while one was open for 6% -> 0% of each run, Pallas kernels for 0% -> 0%
where the time goes in v2:
time: 117 us
  Pallas kernels  112 us (96%)
  other arithmetic  2.77 us (2%)
  local copies, waits for them, and re-layouts  1.24 us (1%)
    pallas_call x1, Pallas kernels, per_device(): pl.pallas_call(functools.partial(layer_kernel, scale_out, names), out_sha...  112 us
    convert_element_type x1, other arithmetic, per_device(): return (grad_input, sums.reshape(8, width, width).astype(F32), gain_sums)  2.77 us

profile of v2, /device:TPU:1, one launch (start us, length us, event | category | flops | bytes accessed | tf_op | source)
XLA Modules:
  0.0 117.2 jit_solution(4588940727251229270)
XLA Ops:
  0.6 112.5 %layer.1 = (bf16[8,32,256]{2,1,0:T(8,128)(2,1)}, bf16[2,32,32,256]{3,2,1,0:T(8,128)(2,1)}, f32[2,256]{1,0:T(2,128)}) custom-call(bf16[8,32,256]{2,1,0:T(8,128)(2,1)} %x_ref.1, bf16[8,32,256]{2,1,0:T(8,128)(2,1)} %up_ref.1, bf16[8,256,256]{2,1,0:T(8,128)(2,1)} %w_ref.1, f32[2,256]{1,0:T(2,128)} %gain_ref.1), custom_call_target="tpu_custom_call" | custom-call | tf_op jit(solution)/shard_map/layer/pallas_call | solution.py:483
  113.1 0.0 copy-start
  113.1 0.0 copy-start.1
  113.1 2.8 %convert.1 = f32[8,256,256]{2,1,0:T(8,128)} convert(bf16[8,256,256]{2,1,0:T(8,128)(2,1)} %bitcast.2) | non-fusion elementwise | flops 524288 | bytes 3145728 | tf_op jit(solution)/shard_map/convert_element_type | solution.py:496
  115.9 0.0 copy-done
  115.9 0.7 copy.9
  116.6 0.0 copy-done.1
  116.6 0.6 copy.10
Async XLA Ops:
  113.1 2.8 %copy-start = (bf16[8,32,256]{2,1,0:T(8,128)(2,1)S(1)}, bf16[8,32,256]{2,1,0:T(8,128)(2,1)}, u32[]{:S(2)}) copy-start(bf16[8,32,256]{2,1,0:T(8,128)(2,1)} %get-tuple-element.12) | copy-start | bytes 393220
  113.1 3.4 %copy-start.1 = (f32[2,256]{1,0:T(2,128)S(1)}, f32[2,256]{1,0:T(2,128)}, u32[]{:S(2)}) copy-start(f32[2,256]{1,0:T(2,128)} %get-tuple-element.14) | copy-start | bytes 6148

commit v3 on v2

v3 whole, which is shorter than its diff:
```python
import functools

import jax
import jax.numpy as jnp
from jax import lax
from jax.experimental import pallas as pl
from jax.experimental.pallas import tpu as pltpu
from jax.sharding import PartitionSpec as P

HEADS = 4
HALF = 64
EPS = 1e-06
MASKED = -1e30
BF = jnp.bfloat16
F32 = jnp.float32
MESH = pl.DeviceIdType.MESH
NEAR = 4
VMEM_SPEC = pl.BlockSpec(memory_space=pltpu.VMEM)


def dot(a, b):
    return lax.dot_general(a, b, (((1,), (0,)), ((), ())), preferred_element_type=F32)


def dot_t(a, b):
    return lax.dot_general(a, b, (((1,), (1,)), ((), ())), preferred_element_type=F32)


def t_dot(a, b):
    return lax.dot_general(a, b, (((0,), (0,)), ((), ())), preferred_element_type=F32)


def unit(rows):
    inverse = lax.rsqrt(jnp.mean(rows * rows, axis=-1, keepdims=True) + EPS)
    return inverse, rows * inverse


def unit_backward(incoming, inverse, unit_rows, gain):
    scaled = incoming * gain
    mean = jnp.mean(scaled * unit_rows, axis=-1, keepdims=True)
    return inverse * (scaled - unit_rows * mean)


class Exchange:
    def __init__(self, count, me, device_of, source_of, target_of, arrivals, sems):
        self.count, self.me, self.device_of = count, me, device_of
        self.source_of, self.target_of, self.arrivals, self.sems = source_of, target_of, arrivals, sems

    def start(self):
        send_sem, recv_sem = self.sems

        def step(k, carry):
            p = lax.rem(self.me + k, self.count)
            pltpu.make_async_remote_copy(
                src_ref=self.source_of(p),
                dst_ref=self.target_of(self.me),
                send_sem=send_sem,
                recv_sem=recv_sem,
                device_id=self.device_of(p),
                device_id_type=MESH,
            ).start()
            return carry

        lax.fori_loop(1, self.count, step, 0)
        self.target_of(self.me)[...] = self.source_of(self.me)[...]

    def wait(self):
        send_sem, recv_sem = self.sems
        copy = pltpu.make_async_remote_copy(
            src_ref=self.arrivals,
            dst_ref=self.arrivals,
            send_sem=send_sem,
            recv_sem=recv_sem,
            device_id=self.device_of(lax.rem(self.me + 1, self.count)),
            device_id_type=MESH,
        )
        copy.wait_recv()
        copy.wait_send()


class ToTime:
    def __init__(self, bins, me, source, target, sems):
        self.bins, self.halo, self.me = bins, bins // 2, me
        self.mine = lax.div(me, bins)
        self.source, self.target, self.sems = source, target, sems

    def copy(self, source, target, half, device):
        return pltpu.make_async_remote_copy(
            src_ref=source,
            dst_ref=target,
            send_sem=self.sems[half],
            recv_sem=self.sems[2],
            device_id={"tm": device},
            device_id_type=MESH,
        )

    def each_half(self, action):
        for half in range(2):
            needed = (self.me < self.bins + self.halo) if half == 0 else (self.me >= self.halo)
            pl.when(needed)(functools.partial(action, half))

    def start(self):
        def send(half):
            def step(k, carry):
                bin_id = lax.rem(self.me + k, self.bins)
                device = bin_id + self.bins * half

                @pl.when(device != self.me)
                def _():
                    slot = self.target.at[self.me - self.halo * half]
                    self.copy(self.source.at[bin_id], slot, half, device).start()

                return carry

            lax.fori_loop(0, self.bins, step, 0)

        self.each_half(send)
        own = self.me - self.halo * self.mine
        self.target[own] = self.source[self.me - self.bins * self.mine]

    def wait(self):
        other = lax.rem(self.me + 1, 2 * self.bins)
        arrivals = self.target.at[pl.ds(0, self.bins + self.halo - 1)]
        self.copy(arrivals, arrivals, 0, other).wait_recv()

        def sent(half):
            @pl.when(self.mine == half)
            def _():
                left = self.source.at[pl.ds(0, self.bins - 1)]
                self.copy(left, left, half, other).wait_send()

            @pl.when(self.mine != half)
            def _():
                self.copy(self.source, self.source, half, other).wait_send()

        self.each_half(sent)


def total(ref, count):
    return lax.fori_loop(1, count, lambda i, acc: acc + ref[i].astype(F32), ref[0].astype(F32))


def swapped(value):
    return jnp.swapaxes(value.astype(F32), 0, 1).astype(BF)


def head_masks(rows, width):
    lane = lax.broadcasted_iota(jnp.int32, (rows, width), 1) // (width // HEADS)
    return [(lane == head).astype(BF) for head in range(HEADS)]


def weights_of(scores):
    e = jnp.exp(scores - jnp.max(scores, axis=0, keepdims=True))
    return e * (1.0 / jnp.sum(e, axis=0, keepdims=True))


def scores_backward(p, dp):
    return (p * (dp - jnp.sum(dp * p, axis=0, keepdims=True))).astype(BF)


def layer_kernel(
    scale_out, names, x_ref, up_ref, gain_ref, w_hbm, gi_ref, sum_ref, gain_out, w_ref, dma, w_sem, *scratch
):
    s = dict(zip(names, scratch))
    frames, bins, width = x_ref.shape
    scale = (width // HEADS) ** (-0.5)
    tm, freq = lax.axis_index("tm"), lax.axis_index("freq")
    plane = s["rs_time"].shape[0]
    tm_count, freq_count = plane // 2 * NEAR, frames
    core, high = lax.rem(freq, 2), lax.div(freq, 2)
    low, column = lax.rem(tm, NEAR), lax.div(tm, NEAR)
    here = column * 2 + core
    far = freq_count // 2
    rows = bins * freq_count
    base = lax.div(tm, bins) * bins

    def in_freq(p):
        return {"freq": p}

    def in_tm(p):
        return {"tm": p}

    def in_half(p):
        return {"tm": base + p}

    def in_plane(p):
        return {"tm": lax.div(p, 2) * NEAR + low, "freq": high * 2 + lax.rem(p, 2)}

    def in_near(p):
        return {"tm": column * NEAR + p, "freq": freq}

    def in_far(p):
        return {"tm": tm, "freq": p * 2 + core}

    used = [0]

    def sems(count=2):
        first = used[0]
        used[0] += count
        return [dma.at[first + i] for i in range(count)]

    def along(group, source_of, target):
        count, me, device_of = group
        arrivals = target.at[pl.ds(0, count - 1)]
        return Exchange(count, me, device_of, source_of, lambda p: target.at[p], arrivals, sems())

    freq_group = (freq_count, freq, in_freq)
    plane_group = (plane, here, in_plane)
    near_group = (NEAR, low, in_near)
    far_group = (far, high, in_far)

    barrier = pltpu.get_barrier_semaphore()

    def tell(first, last, peer_of):
        def step(k, carry):
            pl.semaphore_signal(barrier, inc=1, device_id=peer_of(k), device_id_type=MESH)
            return carry

        lax.fori_loop(first, last, step, 0)

    tell(1, freq_count, lambda k: in_freq(lax.rem(freq + k, freq_count)))
    tell(0, plane // 2, lambda k: in_plane(lax.rem(column + k, plane // 2) * 2 + 1 - core))
    tell(1, tm_count, lambda k: in_tm(lax.rem(tm + k, tm_count)))
    load = pltpu.make_async_copy(w_hbm, w_ref, w_sem)
    load.start()
    s["up_t"][...] = swapped(up_ref[...])
    pl.semaphore_wait(barrier, freq_count - 1 + plane // 2 + tm_count - 1)

    to_frames = along(freq_group, lambda p: x_ref.at[p], s["x_f"])
    to_frames.start()
    up_time = ToTime(bins, tm, s["up_t"], s["up_w"], sems(3))
    up_time.start()
    load.wait()
    to_frames.wait()

    masks = head_masks(rows, width)
    gain = gain_ref[0:1, :]
    x = s["x_f"][...].astype(F32).reshape(rows, width)
    _, unit_rows = unit(x)
    norm = (unit_rows * gain).astype(BF)
    s["n1"][...] = norm
    s["q1"][...] = (dot(norm, w_ref[0]).astype(BF) * scale).astype(BF)
    s["k1"][...] = dot(norm, w_ref[1]).astype(BF)
    s["v1"][...] = dot(norm, w_ref[2]).astype(BF)
    mixed = jnp.zeros((rows, width), F32)
    for head in range(HEADS):
        p = weights_of(dot_t(s["k1"][...], s["q1"][...] * masks[head]))
        s["p1"][head] = p
        mixed = mixed + t_dot(p.astype(BF), s["v1"][...] * masks[head])
    s["o1"][...] = mixed.astype(BF)
    hidden = x + dot(s["o1"][...], w_ref[3])
    s["h_f"][...] = hidden.reshape(x_ref.shape).astype(BF)
    h_back = along(freq_group, lambda p: s["h_f"].at[p], s["h_l"])
    h_back.start()

    up_time.wait()
    blocks, sub = s["up_w"].shape[:2]
    all_rows, own = blocks * sub, bins * sub
    s["up"][...] = s["up_w"][...].astype(F32).reshape(all_rows, width).astype(BF)
    s["go2"][...] = dot_t(s["up"][...], w_ref[7]).astype(BF)
    s["gk2"][...] = jnp.zeros_like(s["gk2"])
    s["gv2"][...] = jnp.zeros_like(s["gv2"])
    h_back.wait()
    s["h_t"][...] = swapped(s["h_l"][...])
    h_time = ToTime(bins, tm, s["h_t"], s["h_w"], sems(3))
    h_time.start()
    h_time.wait()

    gain = gain_ref[1:2, :]
    _, unit_rows = unit(s["h_w"][...].astype(F32).reshape(all_rows, width))
    norm = (unit_rows * gain).astype(BF)
    s["n2"][...] = norm
    s["q2"][...] = (dot(norm, w_ref[4]).astype(BF) * scale).astype(BF)
    s["k2"][...] = dot(norm, w_ref[5]).astype(BF)
    s["v2"][...] = dot(norm, w_ref[6]).astype(BF)
    queries, keys = 2 * HALF, 4 * HALF
    offset = lax.broadcasted_iota(jnp.int32, (keys, queries), 0) - lax.broadcasted_iota(
        jnp.int32, (keys, queries), 1
    )

    def block(i, carry):
        q_at = pl.ds(pl.multiple_of(i * queries, queries), queries)
        k_at = pl.ds(pl.multiple_of(i * HALF, HALF), keys)
        q, go, k, v = s["q2"][q_at, :], s["go2"][q_at, :], s["k2"][k_at, :], s["v2"][k_at, :]
        distance = offset - HALF * i
        allowed = (distance >= -HALF) & (distance < HALF)
        key_masks, query_masks = head_masks(keys, width), head_masks(queries, width)
        mixed = jnp.zeros((queries, width), F32)
        gq = jnp.zeros((queries, width), F32)
        gk = jnp.zeros((keys, width), F32)
        gv = jnp.zeros((keys, width), F32)
        for head in range(HEADS):
            q_head, go_head = q * query_masks[head], go * query_masks[head]
            p = weights_of(jnp.where(allowed, dot_t(k, q_head), MASKED))
            p_half = p.astype(BF)
            ds = scores_backward(p, dot_t(v, go_head))
            mixed = mixed + t_dot(p_half, v * key_masks[head])
            gq = gq + t_dot(ds, k * key_masks[head])
            gk = gk + dot(ds, q_head)
            gv = gv + dot(p_half, go_head)
        s["o2"][q_at, :] = mixed.astype(BF)
        s["gq2"][q_at, :] = (gq * scale).astype(BF)
        s["gk2"][k_at, :] += gk
        s["gv2"][k_at, :] += gv
        return carry

    lax.fori_loop(0, all_rows // queries, block, 0)

    half = lax.div(tm, bins)
    first = pl.multiple_of(half * (own // 2), own // 2)
    at = pl.ds(first, own)
    gq, gk, gv = s["gq2"][at, :], s["gk2"][at, :].astype(BF), s["gv2"][at, :].astype(BF)
    gn = dot_t(gq, w_ref[4]) + dot_t(gk, w_ref[5]) + dot_t(gv, w_ref[6])
    own_blocks = pl.ds(half * (bins // 2), bins)
    inverse, unit_own = unit(s["h_w"][own_blocks].astype(F32).reshape(own, width))
    upstream = s["up"][at, :]
    gh = upstream.astype(F32) + unit_backward(gn, inverse, unit_own, gain)
    s["gh_t"][...] = gh.reshape(bins, sub, width).astype(BF)
    gh_back = along((bins, tm - base, in_half), lambda p: s["gh_t"].at[p], s["gh_b"])
    gh_back.start()

    def place(name, index, value):
        part = (value * scale_out).reshape((plane, width // plane, width)).astype(BF)
        s["wg_" + name][:, index] = part

    def plane_sum(name, index, count):
        stack, target = s["wg_" + name], s["rs_" + name]
        at = pl.ds(index, count)
        arrivals = target.at[pl.ds(0, plane - 1), at]
        return Exchange(
            plane, here, in_plane, lambda p: stack.at[p, at], lambda p: target.at[p, at], arrivals, sems()
        )

    def broadcast(group, name, source):
        return along(group, lambda p: s[source], s[name])

    def later_stages(name, result):
        return [
            broadcast(near_group, "near_" + name, "near_src_" + name),
            broadcast(far_group, "far_" + name, "far_src_" + name),
            along(plane_group, lambda p: s["last_src_" + name], result),
        ]

    def add_up(source, count, target):
        s[target][...] = total(s[source], count).astype(s[target].dtype)

    norm = s["n2"][at, :]
    place("time", 0, t_dot(norm, gq))
    place("time", 1, t_dot(norm, gk))
    place("time", 2, t_dot(norm, gv))
    place("time", 3, t_dot(s["o2"][at, :], upstream))
    s["time_gain"][...] = jnp.sum(gn * unit_own, axis=0, keepdims=True) * scale_out
    t_plane = plane_sum("time", 0, 4)
    t_near, t_far, t_last = later_stages("time", sum_ref.at[1])
    t_plane.start()
    gh_back.wait()
    s["gh_l"][...] = swapped(s["gh_b"][...])
    gh_frames = along(freq_group, lambda p: s["gh_l"].at[p], s["gh_f"])
    gh_frames.start()
    t_plane.wait()
    add_up("rs_time", plane, "near_src_time")
    t_near.start()
    gh_frames.wait()

    f_near, f_far, f_last = later_stages("freq", sum_ref.at[0])
    f_planes = [plane_sum("freq", 3, 1), plane_sum("freq", 2, 1), plane_sum("freq", 0, 2)]
    gh32 = s["gh_f"][...].astype(F32).reshape(rows, width)
    gh = gh32.astype(BF)
    go = dot_t(gh, w_ref[3]).astype(BF)
    place("freq", 3, t_dot(s["o1"][...], gh))
    f_planes[0].start()
    gv = jnp.zeros((rows, width), F32)
    for head in range(HEADS):
        gv = gv + dot(s["p1"][head].astype(BF), go * masks[head])
    gv = gv.astype(BF)
    place("freq", 2, t_dot(s["n1"][...], gv))
    f_planes[1].start()
    gq = jnp.zeros((rows, width), F32)
    gk = jnp.zeros((rows, width), F32)
    for head in range(HEADS):
        ds = scores_backward(s["p1"][head], dot_t(s["v1"][...], go * masks[head]))
        gq = gq + t_dot(ds, s["k1"][...] * masks[head])
        gk = gk + dot(ds, s["q1"][...] * masks[head])
    gq, gk = (gq * scale).astype(BF), gk.astype(BF)
    norm = s["n1"][...]
    place("freq", 0, t_dot(norm, gq))
    place("freq", 1, t_dot(norm, gk))
    f_planes[2].start()
    gain = gain_ref[0:1, :]
    inverse, unit_rows = unit(s["x_f"][...].astype(F32).reshape(rows, width))
    gn = dot_t(gq, w_ref[0]) + dot_t(gk, w_ref[1]) + dot_t(gv, w_ref[2])
    gi = gh32 + unit_backward(gn, inverse, unit_rows, gain)
    s["gi_f"][...] = gi.reshape(x_ref.shape).astype(BF)
    gi_back = along(freq_group, lambda p: s["gi_f"].at[p], gi_ref)
    gi_back.start()

    freq_gain = jnp.sum(gn * unit_rows, axis=0, keepdims=True) * scale_out
    s["g_src_plane"][...] = jnp.concatenate([freq_gain, s["time_gain"][...]], axis=0)
    g_plane = broadcast(plane_group, "g_plane", "g_src_plane")
    g_near = broadcast(near_group, "g_near", "g_src_near")
    g_far = broadcast(far_group, "g_far", "g_src_far")
    g_plane.start()

    t_near.wait()
    add_up("near_time", NEAR, "far_src_time")
    t_far.start()
    for stage in f_planes:
        stage.wait()
    add_up("rs_freq", plane, "near_src_freq")
    f_near.start()
    g_plane.wait()
    add_up("g_plane", plane, "g_src_near")
    g_near.start()
    f_near.wait()
    add_up("near_freq", NEAR, "far_src_freq")
    f_far.start()
    g_near.wait()
    add_up("g_near", NEAR, "g_src_far")
    g_far.start()
    t_far.wait()
    add_up("far_time", far, "last_src_time")
    t_last.start()
    f_far.wait()
    add_up("far_freq", far, "last_src_freq")
    f_last.start()
    g_far.wait()
    gain_out[...] = total(s["g_far"], far)
    gi_back.wait()
    t_last.wait()
    f_last.wait()


def finish_kernel(gi_ref, sum_ref, gain_ref, gi_out, w_out, gain_out):
    plane, count, part, width = sum_ref.shape[1:]
    for index in range(count):
        w_out[index] = sum_ref[0, :, index].astype(F32).reshape(plane * part, width)

    @pl.when(pl.program_id(0) == 0)
    def _():
        gi_out[...] = gi_ref[...]
        gain_out[...] = gain_ref[...]


def per_device(features, upstream, weights, gains):
    frames, bins, width = features.shape
    freq_count, tm_count = lax.axis_size("freq"), lax.axis_size("tm")
    rows = bins * freq_count
    scale_out = (frames * tm_count * rows) ** (-0.5)
    shape = jax.ShapeDtypeStruct
    plane, far = tm_count // NEAR * 2, freq_count // 2
    part = width // plane
    span = bins + bins // 2
    all_rows = span * frames

    local = ((frames, bins, width), BF)
    turned = ((bins, frames, width), BF)
    window = ((span, frames, width), BF)
    flat = ((rows, width), BF)
    tall = ((all_rows, width), BF)
    piece = (4, part, width)
    gain = (2, width)
    buffers = dict(
        up_t=turned, up_w=window, x_f=local, n1=flat, q1=flat, k1=flat, v1=flat, o1=flat,
        p1=((HEADS, rows, rows), F32), h_f=local, h_l=local, h_t=turned, h_w=window,
        up=tall, go2=tall, n2=tall, q2=tall, k2=tall, v2=tall, o2=tall, gq2=tall,
        gk2=((all_rows, width), F32), gv2=((all_rows, width), F32),
        gh_t=turned, gh_b=turned, gh_l=local, gh_f=local, gi_f=local,
        time_gain=((1, width), F32),
        g_src_plane=(gain, F32), g_src_near=(gain, F32), g_src_far=(gain, F32),
        g_plane=((plane,) + gain, F32), g_near=((NEAR,) + gain, F32), g_far=((far,) + gain, F32),
    )
    for name in ("freq", "time"):
        buffers["wg_" + name] = ((plane,) + piece, BF)
        buffers["rs_" + name] = ((plane,) + piece, BF)
        buffers["near_src_" + name] = (piece, BF)
        buffers["near_" + name] = ((NEAR,) + piece, BF)
        buffers["far_src_" + name] = (piece, BF)
        buffers["far_" + name] = ((far,) + piece, BF)
        buffers["last_src_" + name] = (piece, BF)
    names = list(buffers)

    outs = pl.pallas_call(
        functools.partial(layer_kernel, scale_out, names),
        out_shape=[
            shape(features.shape, BF),
            shape((2, plane) + piece, BF),
            shape(gain, F32),
        ],
        in_specs=[VMEM_SPEC] * 3 + [pl.BlockSpec(memory_space=pl.ANY)],
        out_specs=[VMEM_SPEC] * 3,
        scratch_shapes=[
            pltpu.VMEM(weights.shape, BF),
            pltpu.SemaphoreType.DMA((48,)),
            pltpu.SemaphoreType.DMA(()),
        ]
        + [pltpu.VMEM(*buffers[name]) for name in names],
        compiler_params=pltpu.CompilerParams(collective_id=0, has_side_effects=True),
        name="layer",
    )(features, upstream, gains, weights)
    whole = [pl.BlockSpec(features.shape, lambda i: (0, 0, 0)), pl.BlockSpec(gain, lambda i: (0, 0))]
    return pl.pallas_call(
        finish_kernel,
        grid=(2,),
        out_shape=[shape(features.shape, BF), shape(weights.shape, F32), shape(gain, F32)],
        in_specs=[
            whole[0],
            pl.BlockSpec((1, plane) + piece, lambda i: (i, 0, 0, 0, 0)),
            whole[1],
        ],
        out_specs=[whole[0], pl.BlockSpec((4, width, width), lambda i: (i, 0, 0)), whole[1]],
        name="finish",
    )(*outs)


def solution(mesh):
    return jax.shard_map(
        per_device,
        mesh=mesh,
        in_specs=(P("tm", "freq", None), P("tm", "freq", None), P(), P()),
        out_specs=(P("tm", "freq", None), P(), P()),
        check_vma=False,
    )
```

time: 117 us -> 107 us (0.915)
  Pallas kernels: 112 us -> 107 us
  other arithmetic: 2.77 us -> 0 us
  local copies, waits for them, and re-layouts: 1.24 us -> 0 us
    pallas_call x1, Pallas kernels: 112 us -> 104 us  [per_device(): pl.pallas_call(functools.partial(layer_kernel, scale_out, names), out_sha...]
    convert_element_type x1 -> x0, other arithmetic: 2.77 us -> none  [per_device(): return (grad_input, sums.reshape(8, width, width).astype(F32), gain_sums)]
    pallas_call x0 -> x1, Pallas kernels: none -> 2.52 us  [per_device(): pl.pallas_call(finish_kernel, grid=(2,), out_shape=[shape(features.shape,...]
    unnamed x6 -> x0, local copies, waits for them, and re-layouts: 1.24 us -> none
where the time goes in v3:
time: 107 us
  Pallas kernels  107 us (100%)
    pallas_call x1, Pallas kernels, per_device(): pl.pallas_call(functools.partial(layer_kernel, scale_out, names), out_sha...  104 us
    pallas_call x1, Pallas kernels, per_device(): pl.pallas_call(finish_kernel, grid=(2,), out_shape=[shape(features.shape,...  2.52 us

profile of v3, /device:TPU:1, one launch (start us, length us, event | category | flops | bytes accessed | tf_op | source)
XLA Modules:
  0.0 107.2 jit_solution(13643158131576964840)
XLA Ops:
  0.6 104.0 %layer.1 = (bf16[8,32,256]{2,1,0:T(8,128)(2,1)}, bf16[2,32,4,8,256]{4,3,2,1,0:T(8,128)(2,1)}, f32[2,256]{1,0:T(2,128)}) custom-call(bf16[8,32,256]{2,1,0:T(8,128)(2,1)} %x_ref.1, bf16[8,32,256]{2,1,0:T(8,128)(2,1)} %up_ref.1, f32[2,256]{1,0:T(2,128)} %gain_ref.1, bf16[8,256,256]{2,1,0:T(8,128)(2,1)} %w_hbm.1), custom_call_target="tpu_custom_call" | custom-call | tf_op jit(solution)/shard_map/layer/pallas_call | solution.py:482
  104.7 2.5 %finish.1 = (bf16[8,32,256]{2,1,0:T(8,128)(2,1)}, f32[8,256,256]{2,1,0:T(8,128)}, f32[2,256]{1,0:T(2,128)}) custom-call(bf16[8,32,256]{2,1,0:T(8,128)(2,1)} %get-tuple-element.6.gi_ref, bf16[2,32,4,8,256]{4,3,2,1,0:T(8,128)(2,1)} %get-tuple-element.7.sum_ref, f32[2,256]{1,0:T(2,128)} %get-tuple-element.8.gain_ref), custom_call_target="tpu_custom_call" | custom-call | tf_op jit(solution)/shard_map/finish/pallas_call | solution.py:501

commit v4 on v3

--- a/solution.py
+++ b/solution.py
@@ -165,11 +165,11 @@
     frames, bins, width = x_ref.shape
     scale = (width // HEADS) ** (-0.5)
     tm, freq = lax.axis_index("tm"), lax.axis_index("freq")
-    plane = s["rs_time"].shape[0]
-    tm_count, freq_count = plane // 2 * NEAR, frames
+    plane, columns = s["wg_time"].shape[0], s["rs_time"].shape[0]
+    tm_count, freq_count = columns * NEAR, frames
     core, high = lax.rem(freq, 2), lax.div(freq, 2)
     low, column = lax.rem(tm, NEAR), lax.div(tm, NEAR)
-    here = column * 2 + core
+    mine, theirs = core * columns, (1 - core) * columns
     far = freq_count // 2
     rows = bins * freq_count
     base = lax.div(tm, bins) * bins
@@ -183,8 +183,8 @@
     def in_half(p):
         return {"tm": base + p}
 
-    def in_plane(p):
-        return {"tm": lax.div(p, 2) * NEAR + low, "freq": high * 2 + lax.rem(p, 2)}
+    def in_columns(p):
+        return {"tm": p * NEAR + low}
 
     def in_near(p):
         return {"tm": column * NEAR + p, "freq": freq}
@@ -205,7 +205,7 @@
         return Exchange(count, me, device_of, source_of, lambda p: target.at[p], arrivals, sems())
 
     freq_group = (freq_count, freq, in_freq)
-    plane_group = (plane, here, in_plane)
+    column_group = (columns, column, in_columns)
     near_group = (NEAR, low, in_near)
     far_group = (far, high, in_far)
 
@@ -219,12 +219,11 @@
         lax.fori_loop(first, last, step, 0)
 
     tell(1, freq_count, lambda k: in_freq(lax.rem(freq + k, freq_count)))
-    tell(0, plane // 2, lambda k: in_plane(lax.rem(column + k, plane // 2) * 2 + 1 - core))
     tell(1, tm_count, lambda k: in_tm(lax.rem(tm + k, tm_count)))
     load = pltpu.make_async_copy(w_hbm, w_ref, w_sem)
     load.start()
     s["up_t"][...] = swapped(up_ref[...])
-    pl.semaphore_wait(barrier, freq_count - 1 + plane // 2 + tm_count - 1)
+    pl.semaphore_wait(barrier, freq_count - 1 + tm_count - 1)
 
     to_frames = along(freq_group, lambda p: x_ref.at[p], s["x_f"])
     to_frames.start()
@@ -323,22 +322,37 @@
         part = (value * scale_out).reshape((plane, width // plane, width)).astype(BF)
         s["wg_" + name][:, index] = part
 
-    def plane_sum(name, index, count):
-        stack, target = s["wg_" + name], s["rs_" + name]
+    def to_partner(source, target):
+        send_sem, recv_sem = sems()
+        return pltpu.make_async_remote_copy(
+            src_ref=source,
+            dst_ref=target,
+            send_sem=send_sem,
+            recv_sem=recv_sem,
+            device_id={"freq": freq + 1 - 2 * core},
+            device_id_type=MESH,
+        )
+
+    def halve(name, index, count):
         at = pl.ds(index, count)
-        arrivals = target.at[pl.ds(0, plane - 1), at]
-        return Exchange(
-            plane, here, in_plane, lambda p: stack.at[p, at], lambda p: target.at[p, at], arrivals, sems()
-        )
+        return to_partner(s["wg_" + name].at[pl.ds(theirs, columns), at], s["pair_" + name].at[:, at])
+
+    def add_pair(name, index, count):
+        at = pl.ds(index, count)
+        own = s["wg_" + name][pl.ds(mine, columns), at].astype(F32)
+        s["both_" + name][:, at] = (own + s["pair_" + name][:, at].astype(F32)).astype(BF)
 
     def broadcast(group, name, source):
         return along(group, lambda p: s[source], s[name])
 
     def later_stages(name, result):
+        part = result.at[pl.ds(mine, columns)]
         return [
+            along(column_group, lambda p: s["both_" + name].at[p], s["rs_" + name]),
             broadcast(near_group, "near_" + name, "near_src_" + name),
             broadcast(far_group, "far_" + name, "far_src_" + name),
-            along(plane_group, lambda p: s["last_src_" + name], result),
+            along(column_group, lambda p: s["last_src_" + name], part),
+            to_partner(part, part),
         ]
 
     def add_up(source, count, target):
@@ -350,31 +364,36 @@
     place("time", 2, t_dot(norm, gv))
     place("time", 3, t_dot(s["o2"][at, :], upstream))
     s["time_gain"][...] = jnp.sum(gn * unit_own, axis=0, keepdims=True) * scale_out
-    t_plane = plane_sum("time", 0, 4)
-    t_near, t_far, t_last = later_stages("time", sum_ref.at[1])
+    t_pair = halve("time", 0, 4)
+    t_plane, t_near, t_far, t_last, t_out = later_stages("time", sum_ref.at[1])
+    t_pair.start()
+    t_pair.wait()
+    add_pair("time", 0, 4)
     t_plane.start()
     gh_back.wait()
     s["gh_l"][...] = swapped(s["gh_b"][...])
     gh_frames = along(freq_group, lambda p: s["gh_l"].at[p], s["gh_f"])
     gh_frames.start()
     t_plane.wait()
-    add_up("rs_time", plane, "near_src_time")
+    add_up("rs_time", columns, "near_src_time")
     t_near.start()
+    t_near.wait()
+    add_up("near_time", NEAR, "far_src_time")
+    t_far.start()
     gh_frames.wait()
 
-    f_near, f_far, f_last = later_stages("freq", sum_ref.at[0])
-    f_planes = [plane_sum("freq", 3, 1), plane_sum("freq", 2, 1), plane_sum("freq", 0, 2)]
+    f_pairs = [halve("freq", 3, 2), halve("freq", 0, 3)]
+    f_plane, f_near, f_far, f_last, f_out = later_stages("freq", sum_ref.at[0])
     gh32 = s["gh_f"][...].astype(F32).reshape(rows, width)
     gh = gh32.astype(BF)
     go = dot_t(gh, w_ref[3]).astype(BF)
-    place("freq", 3, t_dot(s["o1"][...], gh))
-    f_planes[0].start()
+    place("freq", 4, t_dot(s["o1"][...], gh))
     gv = jnp.zeros((rows, width), F32)
     for head in range(HEADS):
         gv = gv + dot(s["p1"][head].astype(BF), go * masks[head])
     gv = gv.astype(BF)
-    place("freq", 2, t_dot(s["n1"][...], gv))
-    f_planes[1].start()
+    place("freq", 3, t_dot(s["n1"][...], gv))
+    f_pairs[0].start()
     gq = jnp.zeros((rows, width), F32)
     gk = jnp.zeros((rows, width), F32)
     for head in range(HEADS):
@@ -383,51 +402,48 @@
         gk = gk + dot(ds, s["q1"][...] * masks[head])
     gq, gk = (gq * scale).astype(BF), gk.astype(BF)
     norm = s["n1"][...]
-    place("freq", 0, t_dot(norm, gq))
-    place("freq", 1, t_dot(norm, gk))
-    f_planes[2].start()
+    place("freq", 1, t_dot(norm, gq))
+    place("freq", 2, t_dot(norm, gk))
     gain = gain_ref[0:1, :]
     inverse, unit_rows = unit(s["x_f"][...].astype(F32).reshape(rows, width))
     gn = dot_t(gq, w_ref[0]) + dot_t(gk, w_ref[1]) + dot_t(gv, w_ref[2])
+    freq_gain = jnp.sum(gn * unit_rows, axis=0, keepdims=True) * scale_out
+    gain_rows = jnp.concatenate(
+        [freq_gain, s["time_gain"][...], jnp.zeros((width // plane - 2, width), F32)], axis=0
+    )
+    s["wg_freq"][:, 0] = jnp.broadcast_to(gain_rows[None], (plane,) + gain_rows.shape).astype(BF)
+    f_pairs[1].start()
+    f_pairs[0].wait()
+    add_pair("freq", 3, 2)
     gi = gh32 + unit_backward(gn, inverse, unit_rows, gain)
     s["gi_f"][...] = gi.reshape(x_ref.shape).astype(BF)
+    f_pairs[1].wait()
+    add_pair("freq", 0, 3)
+    f_plane.start()
     gi_back = along(freq_group, lambda p: s["gi_f"].at[p], gi_ref)
     gi_back.start()
 
-    freq_gain = jnp.sum(gn * unit_rows, axis=0, keepdims=True) * scale_out
-    s["g_src_plane"][...] = jnp.concatenate([freq_gain, s["time_gain"][...]], axis=0)
-    g_plane = broadcast(plane_group, "g_plane", "g_src_plane")
-    g_near = broadcast(near_group, "g_near", "g_src_near")
-    g_far = broadcast(far_group, "g_far", "g_src_far")
-    g_plane.start()
-
-    t_near.wait()
-    add_up("near_time", NEAR, "far_src_time")
-    t_far.start()
-    for stage in f_planes:
-        stage.wait()
-    add_up("rs_freq", plane, "near_src_freq")
+    f_plane.wait()
+    add_up("rs_freq", columns, "near_src_freq")
     f_near.start()
-    g_plane.wait()
-    add_up("g_plane", plane, "g_src_near")
-    g_near.start()
+    t_far.wait()
+    add_up("far_time", far, "last_src_time")
+    t_last.start()
     f_near.wait()
     add_up("near_freq", NEAR, "far_src_freq")
     f_far.start()
-    g_near.wait()
-    add_up("g_near", NEAR, "g_src_far")
-    g_far.start()
-    t_far.wait()
-    add_up("far_time", far, "last_src_time")
-    t_last.start()
+    t_last.wait()
+    t_out.start()
     f_far.wait()
-    add_up("far_freq", far, "last_src_freq")
+    sums = total(s["far_freq"], far)
+    s["last_src_freq"][...] = sums[1:].astype(BF)
     f_last.start()
-    g_far.wait()
-    gain_out[...] = total(s["g_far"], far)
+    gain_out[...] = sums[0, 0:2]
     gi_back.wait()
-    t_last.wait()
     f_last.wait()
+    f_out.start()
+    t_out.wait()
+    f_out.wait()
 
 
 def finish_kernel(gi_ref, sum_ref, gain_ref, gi_out, w_out, gain_out):
@@ -466,16 +482,16 @@
         gk2=((all_rows, width), F32), gv2=((all_rows, width), F32),
         gh_t=turned, gh_b=turned, gh_l=local, gh_f=local, gi_f=local,
         time_gain=((1, width), F32),
-        g_src_plane=(gain, F32), g_src_near=(gain, F32), g_src_far=(gain, F32),
-        g_plane=((plane,) + gain, F32), g_near=((NEAR,) + gain, F32), g_far=((far,) + gain, F32),
     )
-    for name in ("freq", "time"):
-        buffers["wg_" + name] = ((plane,) + piece, BF)
-        buffers["rs_" + name] = ((plane,) + piece, BF)
-        buffers["near_src_" + name] = (piece, BF)
-        buffers["near_" + name] = ((NEAR,) + piece, BF)
-        buffers["far_src_" + name] = (piece, BF)
-        buffers["far_" + name] = ((far,) + piece, BF)
+    for name, pieces in (("freq", 5), ("time", 4)):
+        stack = (pieces, part, width)
+        buffers["wg_" + name] = ((plane,) + stack, BF)
+        for step in ("pair_", "both_", "rs_"):
+            buffers[step + name] = ((plane // 2,) + stack, BF)
+        buffers["near_src_" + name] = (stack, BF)
+        buffers["near_" + name] = ((NEAR,) + stack, BF)
+        buffers["far_src_" + name] = (stack, BF)
+        buffers["far_" + name] = ((far,) + stack, BF)
         buffers["last_src_" + name] = (piece, BF)
     names = list(buffers)
 

time: 107 us -> 105 us (0.981)
  Pallas kernels: 107 us -> 104 us
    pallas_call x1, Pallas kernels: 104 us -> 102 us  [per_device(): pl.pallas_call(functools.partial(layer_kernel, scale_out, names), out_sha...]
where the time goes in v4:
time: 105 us
  Pallas kernels  104 us (99%)
    pallas_call x1, Pallas kernels, per_device(): pl.pallas_call(functools.partial(layer_kernel, scale_out, names), out_sha...  102 us
    pallas_call x1, Pallas kernels, per_device(): pl.pallas_call(finish_kernel, grid=(2,), out_shape=[shape(features.shape,...  2.52 us

profile of v4, /device:TPU:1, one launch (start us, length us, event | category | flops | bytes accessed | tf_op | source)
XLA Modules:
  0.0 104.9 jit_solution(4941091479759381201)
XLA Ops:
  0.6 101.8 %layer.1 = (bf16[8,32,256]{2,1,0:T(8,128)(2,1)}, bf16[2,32,4,8,256]{4,3,2,1,0:T(8,128)(2,1)}, f32[2,256]{1,0:T(2,128)}) custom-call(bf16[8,32,256]{2,1,0:T(8,128)(2,1)} %x_ref.1, bf16[8,32,256]{2,1,0:T(8,128)(2,1)} %up_ref.1, f32[2,256]{1,0:T(2,128)} %gain_ref.1, bf16[8,256,256]{2,1,0:T(8,128)(2,1)} %w_hbm.1), custom_call_target="tpu_custom_call" | custom-call | tf_op jit(solution)/shard_map/layer/pallas_call | solution.py:498
  102.4 2.5 %finish.1 = (bf16[8,32,256]{2,1,0:T(8,128)(2,1)}, f32[8,256,256]{2,1,0:T(8,128)}, f32[2,256]{1,0:T(2,128)}) custom-call(bf16[8,32,256]{2,1,0:T(8,128)(2,1)} %get-tuple-element.6.gi_ref, bf16[2,32,4,8,256]{4,3,2,1,0:T(8,128)(2,1)} %get-tuple-element.7.sum_ref, f32[2,256]{1,0:T(2,128)} %get-tuple-element.8.gain_ref), custom_call_target="tpu_custom_call" | custom-call | tf_op jit(solution)/shard_map/finish/pallas_call | solution.py:517

commit v5 on v4

--- a/solution.py
+++ b/solution.py
@@ -14,6 +14,7 @@
 BF = jnp.bfloat16
 F32 = jnp.float32
 MESH = pl.DeviceIdType.MESH
+SEMAPHORES = 42
 NEAR = 4
 VMEM_SPEC = pl.BlockSpec(memory_space=pltpu.VMEM)
 
@@ -159,7 +160,8 @@
 
 
 def layer_kernel(
-    scale_out, names, x_ref, up_ref, gain_ref, w_hbm, gi_ref, sum_ref, gain_out, w_ref, dma, w_sem, *scratch
+    scale_out, names, x_hbm, up_hbm, gain_hbm, w_hbm, gi_ref, sum_ref, gain_out,
+    x_ref, up_ref, gain_ref, w_ref, dma, load_sem, *scratch
 ):
     s = dict(zip(names, scratch))
     frames, bins, width = x_ref.shape
@@ -209,6 +211,11 @@
     near_group = (NEAR, low, in_near)
     far_group = (far, high, in_far)
 
+    pairs = ((x_hbm, x_ref), (up_hbm, up_ref), (gain_hbm, gain_ref), (w_hbm, w_ref))
+    loads = [pltpu.make_async_copy(a, b, load_sem.at[i]) for i, (a, b) in enumerate(pairs)]
+    for load in loads:
+        load.start()
+
     barrier = pltpu.get_barrier_semaphore()
 
     def tell(first, last, peer_of):
@@ -220,8 +227,8 @@
 
     tell(1, freq_count, lambda k: in_freq(lax.rem(freq + k, freq_count)))
     tell(1, tm_count, lambda k: in_tm(lax.rem(tm + k, tm_count)))
-    load = pltpu.make_async_copy(w_hbm, w_ref, w_sem)
-    load.start()
+    for load in loads[:3]:
+        load.wait()
     s["up_t"][...] = swapped(up_ref[...])
     pl.semaphore_wait(barrier, freq_count - 1 + tm_count - 1)
 
@@ -229,7 +236,7 @@
     to_frames.start()
     up_time = ToTime(bins, tm, s["up_t"], s["up_w"], sems(3))
     up_time.start()
-    load.wait()
+    loads[3].wait()
     to_frames.wait()
 
     masks = head_masks(rows, width)
@@ -444,6 +451,7 @@
     f_out.start()
     t_out.wait()
     f_out.wait()
+    assert used[0] <= SEMAPHORES, used
 
 
 def finish_kernel(gi_ref, sum_ref, gain_ref, gi_out, w_out, gain_out):
@@ -502,12 +510,15 @@
             shape((2, plane) + piece, BF),
             shape(gain, F32),
         ],
-        in_specs=[VMEM_SPEC] * 3 + [pl.BlockSpec(memory_space=pl.ANY)],
+        in_specs=[pl.BlockSpec(memory_space=pl.ANY)] * 4,
         out_specs=[VMEM_SPEC] * 3,
         scratch_shapes=[
+            pltpu.VMEM(features.shape, BF),
+            pltpu.VMEM(upstream.shape, BF),
+            pltpu.VMEM(gain, F32),
             pltpu.VMEM(weights.shape, BF),
-            pltpu.SemaphoreType.DMA((48,)),
-            pltpu.SemaphoreType.DMA(()),
+            pltpu.SemaphoreType.DMA((SEMAPHORES,)),
+            pltpu.SemaphoreType.DMA((4,)),
         ]
         + [pltpu.VMEM(*buffers[name]) for name in names],
         compiler_params=pltpu.CompilerParams(collective_id=0, has_side_effects=True),

time: 105 us -> 104 us (level)
    pallas_call x1, Pallas kernels: 102 us -> 100 us  [per_device(): pl.pallas_call(functools.partial(layer_kernel, scale_out, names), out_sha...]
where the time goes in v5:
time: 104 us; the launch traced here: 103 us
  Pallas kernels  103 us (99%)
    pallas_call x1, Pallas kernels, per_device(): pl.pallas_call(functools.partial(layer_kernel, scale_out, names), out_sha...  100 us
    pallas_call x1, Pallas kernels, per_device(): pl.pallas_call(finish_kernel, grid=(2,), out_shape=[shape(features.shape,...  2.52 us

profile of v5, /device:TPU:1, one launch (start us, length us, event | category | flops | bytes accessed | tf_op | source)
XLA Modules:
  0.0 103.5 jit_solution(103039650878467605)
XLA Ops:
  0.6 100.3 %layer.1 = (bf16[8,32,256]{2,1,0:T(8,128)(2,1)}, bf16[2,32,4,8,256]{4,3,2,1,0:T(8,128)(2,1)}, f32[2,256]{1,0:T(2,128)}) custom-call(bf16[8,32,256]{2,1,0:T(8,128)(2,1)} %x_hbm.1, bf16[8,32,256]{2,1,0:T(8,128)(2,1)} %up_hbm.1, f32[2,256]{1,0:T(2,128)} %gain_hbm.1, bf16[8,256,256]{2,1,0:T(8,128)(2,1)} %w_hbm.1), custom_call_target="tpu_custom_call" | custom-call | tf_op jit(solution)/shard_map/layer/pallas_call | solution.py:506
  100.9 2.5 %finish.1 = (bf16[8,32,256]{2,1,0:T(8,128)(2,1)}, f32[8,256,256]{2,1,0:T(8,128)}, f32[2,256]{1,0:T(2,128)}) custom-call(bf16[8,32,256]{2,1,0:T(8,128)(2,1)} %get-tuple-element.6.gi_ref, bf16[2,32,4,8,256]{4,3,2,1,0:T(8,128)(2,1)} %get-tuple-element.7.sum_ref, f32[2,256]{1,0:T(2,128)} %get-tuple-element.8.gain_ref), custom_call_target="tpu_custom_call" | custom-call | tf_op jit(solution)/shard_map/finish/pallas_call | solution.py:528

commit v6 on v5

--- a/solution.py
+++ b/solution.py
@@ -63,6 +63,30 @@
             return carry
 
         lax.fori_loop(1, self.count, step, 0)
+        self.target_of(self.me)[...] = self.source_of(self.me)[...]
+
+    def start_range(self, first, count):
+        send_sem, recv_sem = self.sems
+
+        def step(k, carry):
+            p = first + lax.rem(self.me + k, count)
+
+            @pl.when(p != self.me)
+            def _():
+                pltpu.make_async_remote_copy(
+                    src_ref=self.source_of(p),
+                    dst_ref=self.target_of(self.me),
+                    send_sem=send_sem,
+                    recv_sem=recv_sem,
+                    device_id=self.device_of(p),
+                    device_id_type=MESH,
+                ).start()
+
+            return carry
+
+        lax.fori_loop(0, count, step, 0)
+
+    def keep(self):
         self.target_of(self.me)[...] = self.source_of(self.me)[...]
 
     def wait(self):
@@ -284,7 +308,10 @@
         jnp.int32, (keys, queries), 1
     )
 
-    def block(i, carry):
+    half = lax.div(tm, bins)
+
+    def block(n, carry):
+        i = n + half * (all_rows // queries - 1 - 2 * n)
         q_at = pl.ds(pl.multiple_of(i * queries, queries), queries)
         k_at = pl.ds(pl.multiple_of(i * HALF, HALF), keys)
         q, go, k, v = s["q2"][q_at, :], s["go2"][q_at, :], s["k2"][k_at, :], s["v2"][k_at, :]
@@ -310,20 +337,32 @@
         s["gv2"][k_at, :] += gv
         return carry
 
-    lax.fori_loop(0, all_rows // queries, block, 0)
-
-    half = lax.div(tm, bins)
-    first = pl.multiple_of(half * (own // 2), own // 2)
-    at = pl.ds(first, own)
+    gh_back = along((bins, tm - base, in_half), lambda p: s["gh_t"].at[p], s["gh_b"])
+    first = half * (bins // 2)
+
+    def finish(part):
+        many = own // 2
+        some = many // sub
+        skip = (part + half * (1 - 2 * part)) * some
+        mine_at = pl.ds(skip, some)
+        at = pl.ds(pl.multiple_of((first + skip) * sub, many), many)
+        gq, gk, gv = s["gq2"][at, :], s["gk2"][at, :].astype(BF), s["gv2"][at, :].astype(BF)
+        gn = dot_t(gq, w_ref[4]) + dot_t(gk, w_ref[5]) + dot_t(gv, w_ref[6])
+        inverse, unit_own = unit(s["h_w"][pl.ds(first + skip, some)].astype(F32).reshape(many, width))
+        gh = s["up"][at, :].astype(F32) + unit_backward(gn, inverse, unit_own, gain)
+        s["gh_t"][mine_at] = gh.reshape(some, sub, width).astype(BF)
+        sums = jnp.sum(gn * unit_own, axis=0, keepdims=True) * scale_out
+        s["time_gain"][...] = sums if part == 0 else s["time_gain"][...] + sums
+        gh_back.start_range(skip, some)
+
+    lax.fori_loop(0, all_rows // queries - 1, block, 0)
+    finish(0)
+    block(all_rows // queries - 1, 0)
+    finish(1)
+    gh_back.keep()
+    at = pl.ds(pl.multiple_of(first * sub, own // 2), own)
+    upstream = s["up"][at, :]
     gq, gk, gv = s["gq2"][at, :], s["gk2"][at, :].astype(BF), s["gv2"][at, :].astype(BF)
-    gn = dot_t(gq, w_ref[4]) + dot_t(gk, w_ref[5]) + dot_t(gv, w_ref[6])
-    own_blocks = pl.ds(half * (bins // 2), bins)
-    inverse, unit_own = unit(s["h_w"][own_blocks].astype(F32).reshape(own, width))
-    upstream = s["up"][at, :]
-    gh = upstream.astype(F32) + unit_backward(gn, inverse, unit_own, gain)
-    s["gh_t"][...] = gh.reshape(bins, sub, width).astype(BF)
-    gh_back = along((bins, tm - base, in_half), lambda p: s["gh_t"].at[p], s["gh_b"])
-    gh_back.start()
 
     def place(name, index, value):
         part = (value * scale_out).reshape((plane, width // plane, width)).astype(BF)
@@ -370,7 +409,6 @@
     place("time", 1, t_dot(norm, gk))
     place("time", 2, t_dot(norm, gv))
     place("time", 3, t_dot(s["o2"][at, :], upstream))
-    s["time_gain"][...] = jnp.sum(gn * unit_own, axis=0, keepdims=True) * scale_out
     t_pair = halve("time", 0, 4)
     t_plane, t_near, t_far, t_last, t_out = later_stages("time", sum_ref.at[1])
     t_pair.start()

time: 104 us -> 105 us (level)
    pallas_call x1, Pallas kernels: 100 us -> 102 us  [per_device(): pl.pallas_call(functools.partial(layer_kernel, scale_out, names), out_sha...]
where the time goes in v6:
time: 105 us
  Pallas kernels  104 us (99%)
    pallas_call x1, Pallas kernels, per_device(): pl.pallas_call(functools.partial(layer_kernel, scale_out, names), out_sha...  102 us
    pallas_call x1, Pallas kernels, per_device(): pl.pallas_call(finish_kernel, grid=(2,), out_shape=[shape(features.shape,...  2.52 us

profile of v6, /device:TPU:1, one launch (start us, length us, event | category | flops | bytes accessed | tf_op | source)
XLA Modules:
  0.0 104.8 jit_solution(13287457793986662589)
XLA Ops:
  0.6 101.6 %layer.1 = (bf16[8,32,256]{2,1,0:T(8,128)(2,1)}, bf16[2,32,4,8,256]{4,3,2,1,0:T(8,128)(2,1)}, f32[2,256]{1,0:T(2,128)}) custom-call(bf16[8,32,256]{2,1,0:T(8,128)(2,1)} %x_hbm.1, bf16[8,32,256]{2,1,0:T(8,128)(2,1)} %up_hbm.1, f32[2,256]{1,0:T(2,128)} %gain_hbm.1, bf16[8,256,256]{2,1,0:T(8,128)(2,1)} %w_hbm.1), custom_call_target="tpu_custom_call" | custom-call | tf_op jit(solution)/shard_map/layer/pallas_call | solution.py:544
  102.3 2.5 %finish.1 = (bf16[8,32,256]{2,1,0:T(8,128)(2,1)}, f32[8,256,256]{2,1,0:T(8,128)}, f32[2,256]{1,0:T(2,128)}) custom-call(bf16[8,32,256]{2,1,0:T(8,128)(2,1)} %get-tuple-element.6.gi_ref, bf16[2,32,4,8,256]{4,3,2,1,0:T(8,128)(2,1)} %get-tuple-element.7.sum_ref, f32[2,256]{1,0:T(2,128)} %get-tuple-element.8.gain_ref), custom_call_target="tpu_custom_call" | custom-call | tf_op jit(solution)/shard_map/finish/pallas_call | solution.py:566

commit v7 on v5

--- a/solution.py
+++ b/solution.py
@@ -454,15 +454,32 @@
     assert used[0] <= SEMAPHORES, used
 
 
-def finish_kernel(gi_ref, sum_ref, gain_ref, gi_out, w_out, gain_out):
-    plane, count, part, width = sum_ref.shape[1:]
-    for index in range(count):
-        w_out[index] = sum_ref[0, :, index].astype(F32).reshape(plane * part, width)
-
-    @pl.when(pl.program_id(0) == 0)
-    def _():
-        gi_out[...] = gi_ref[...]
-        gain_out[...] = gain_ref[...]
+def finish_kernel(gi_hbm, sum_hbm, gain_hbm, gi_out, w_out, gain_out, gi, sums, gain, whole, come, leave):
+    sets, plane, count, part, width = sums.shape
+    loads = [pltpu.make_async_copy(sum_hbm.at[i], sums.at[i], come.at[i]) for i in range(sets)]
+    small = [
+        pltpu.make_async_copy(gi_hbm, gi, come.at[sets]),
+        pltpu.make_async_copy(gain_hbm, gain, come.at[sets + 1]),
+    ]
+    stores = [
+        pltpu.make_async_copy(gi, gi_out, leave.at[0]),
+        pltpu.make_async_copy(gain, gain_out, leave.at[1]),
+    ]
+    for copy in loads + small:
+        copy.start()
+    for i in range(sets):
+        loads[i].wait()
+        for j in range(count):
+            m = i * count + j
+            whole[m] = sums[i, :, j].astype(F32).reshape(plane * part, width)
+            stores.append(pltpu.make_async_copy(whole.at[m], w_out.at[m], leave.at[2 + m]))
+            stores[-1].start()
+        if i == 0:
+            for load, store in zip(small, stores[:2]):
+                load.wait()
+                store.start()
+    for store in stores:
+        store.wait()
 
 
 def per_device(features, upstream, weights, gains):
@@ -524,17 +541,20 @@
         compiler_params=pltpu.CompilerParams(collective_id=0, has_side_effects=True),
         name="layer",
     )(features, upstream, gains, weights)
-    whole = [pl.BlockSpec(features.shape, lambda i: (0, 0, 0)), pl.BlockSpec(gain, lambda i: (0, 0))]
+    anywhere = pl.BlockSpec(memory_space=pl.ANY)
     return pl.pallas_call(
         finish_kernel,
-        grid=(2,),
         out_shape=[shape(features.shape, BF), shape(weights.shape, F32), shape(gain, F32)],
-        in_specs=[
-            whole[0],
-            pl.BlockSpec((1, plane) + piece, lambda i: (i, 0, 0, 0, 0)),
-            whole[1],
+        in_specs=[anywhere] * 3,
+        out_specs=[anywhere] * 3,
+        scratch_shapes=[
+            pltpu.VMEM(features.shape, BF),
+            pltpu.VMEM((2, plane) + piece, BF),
+            pltpu.VMEM(gain, F32),
+            pltpu.VMEM(weights.shape, F32),
+            pltpu.SemaphoreType.DMA((4,)),
+            pltpu.SemaphoreType.DMA((10,)),
         ],
-        out_specs=[whole[0], pl.BlockSpec((4, width, width), lambda i: (i, 0, 0)), whole[1]],
         name="finish",
     )(*outs)
 

time: 104 us -> 104 us (level)
  no operation moved by 1% of the time
where the time goes in v7:
time: 104 us; the launch traced here: 103 us
  Pallas kernels  103 us (99%)
    pallas_call x1, Pallas kernels, per_device(): pl.pallas_call(functools.partial(layer_kernel, scale_out, names), out_sha...  100 us
    pallas_call x1, Pallas kernels, per_device(): pl.pallas_call(finish_kernel, out_shape=[shape(features.shape, BF), shape...  2.53 us

profile of v7, /device:TPU:1, one launch (start us, length us, event | category | flops | bytes accessed | tf_op | source)
XLA Modules:
  0.0 103.5 jit_solution(9487787515921863039)
XLA Ops:
  0.6 100.3 %layer.1 = (bf16[8,32,256]{2,1,0:T(8,128)(2,1)}, bf16[2,32,4,8,256]{4,3,2,1,0:T(8,128)(2,1)}, f32[2,256]{1,0:T(2,128)}) custom-call(bf16[8,32,256]{2,1,0:T(8,128)(2,1)} %x_hbm.1, bf16[8,32,256]{2,1,0:T(8,128)(2,1)} %up_hbm.1, f32[2,256]{1,0:T(2,128)} %gain_hbm.1, bf16[8,256,256]{2,1,0:T(8,128)(2,1)} %w_hbm.1), custom_call_target="tpu_custom_call" | custom-call | tf_op jit(solution)/shard_map/layer/pallas_call | solution.py:523
  100.9 2.5 %finish.1 = (bf16[8,32,256]{2,1,0:T(8,128)(2,1)}, f32[8,256,256]{2,1,0:T(8,128)}, f32[2,256]{1,0:T(2,128)}) custom-call(bf16[8,32,256]{2,1,0:T(8,128)(2,1)} %get-tuple-element.6.gi_hbm, bf16[2,32,4,8,256]{4,3,2,1,0:T(8,128)(2,1)} %get-tuple-element.7.sum_hbm, f32[2,256]{1,0:T(2,128)} %get-tuple-element.8.gain_hbm), custom_call_target="tpu_custom_call" | custom-call | tf_op jit(solution)/shard_map/finish/pallas_call | solution.py:545
